TPU v7x, 32 devices: a whole 2x2x4 slice. The times are simulated.
32 devices in a mesh: ctx: 16 (over z, y, x), head: 2 (over core).
Axes of the slice: x: 2, y: 2, z: 4, core: 2. Of those that a mesh axis runs over, the one named last changes fastest.
Arguments:
- queries: bfloat16 [4096, 16, 128], P('ctx', 'head'), may hold values from -6 to 6
- key_vecs: bfloat16 [4096, 16, 128], P('ctx', 'head'), may hold values from -16 to 16
- values: bfloat16 [4096, 16, 128], P('ctx', 'head'), may hold values from -6 to 6
- log_decay: float32 [16, 4096], P('head', 'ctx'), may hold values from -1.5 to 0
- ridge_diag: float32 [16, 128], P('head'), may hold values from 0.05 to 1
- residual: bfloat16 [4096, 2048], P(('ctx', 'head')), may hold values from -6 to 6
- w_out: bfloat16 [2048, 2048], P('head'), may hold values from -0.125 to 0.125
- norm_gain: float32 [2048], replicated, may hold values from 0.1 to 1.9
- routes: int32 [4096, 8], P(('ctx', 'head')), may hold values from 0 to 31, as said below
- gate_probs: float32 [4096, 8], P(('ctx', 'head')), may hold values from 0.1 to 0.5
- w_gate: bfloat16 [32, 2048, 768], P(('ctx', 'head')), may hold values from -0.125 to 0.125
- w_up: bfloat16 [32, 2048, 768], P(('ctx', 'head')), may hold values from -0.125 to 0.125
- w_down: bfloat16 [32, 768, 2048], P(('ctx', 'head')), may hold values from -0.21875 to 0.21875
Outputs:
- attended: bfloat16 [4096, 2048], P(('ctx', 'head'))
- layer_out: bfloat16 [4096, 2048], P(('ctx', 'head'))
Inputs may be any that keep to these rules, and one draw needn't show every extreme that they name: `routes`: the k-th route of every token names an expert of group k, the experts k * 4 to (k + 1) * 4 - 1. In every aligned block of 128 tokens (the tokens of one device) no expert is named more than 64 times, and in every group one expert is named exactly 64 times in every block.
All inputs are finite; a program needn't handle non-finite values.
Results may differ from a plain program's by a relative error of at most 0.012.
Values may be sent and summed in bfloat16 or wider, within the bound.
No kernel may reach another device: no remote copies, remote signals or barrier semaphores. Data moves between devices by JAX's collectives and lax.ppermute only.
A program may use at most 192 MiB of HBM per device.

v0:
```python
import functools

import jax
import jax.numpy as jnp
from jax import lax
from jax.experimental import pallas as pl
from jax.experimental.pallas import tpu as pltpu
from jax.sharding import PartitionSpec as P

CG_STEPS = 4

norm_eps = 1e-06
BOTH = ("ctx", "head")


def grid_dims(count):
    bits = count.bit_length() - 1
    if 1 << bits != count:
        return (count, 1, 1)
    first = -(-bits // 3)
    second = -(-(bits - first) // 2)
    return (1 << first, 1 << second, 1 << (bits - first - second))


def shifted(place, dims, dim, by):
    coords = [place // (dims[1] * dims[2]), place // dims[2] % dims[1], place % dims[2]]
    coords[dim] = (coords[dim] + by) % dims[dim]
    return (coords[0] * dims[1] + coords[1]) * dims[2] + coords[2]


def phase_dims(dims):
    if dims[1] == dims[2]:
        return ((0, 2, 1), (0, 1, 2))
    return ((0, 2, 1), (0, 2, 1))


def hop(block, dims, n_head, phase, by):
    orders = phase_dims(dims)
    count = dims[0] * dims[1] * dims[2]
    pairs = []
    for place in range(count):
        for core in range(n_head):
            dest = shifted(place, dims, orders[core % 2][phase], by)
            pairs.append((place * n_head + core, dest * n_head + core))
    return lax.ppermute(block, BOTH, pairs)


def slot_sizes(dims):
    order = phase_dims(dims)[0]
    return tuple(dims[d] for d in order)


def spread(block, dims, n_head):
    s0, sa, sb = slot_sizes(dims)
    heads = [block]
    for r0 in visit(s0)[1:]:
        heads.append(hop(block, dims, n_head, 0, r0))
    groups = {}
    for r0, head in zip(visit(s0), heads, strict=True):
        line = [head]
        for ra in range(1, sa):
            line.append(hop(head, dims, n_head, 1, ra))
        group = [line]
        for rb in range(1, sb):
            group.append([hop(one, dims, n_head, 2, rb) for one in line])
        groups[r0] = group
    return groups


def visit(size):
    return [0] + sorted(range(1, size), key=lambda r: (-min(r, size - r), r))


def add_all(first, others, dtype):
    total = first.astype(jnp.float32)
    for other in others:
        total = total + other.astype(jnp.float32)
    return total.astype(dtype)


def collect(outs, r0, dims, n_head):
    _, sa, sb = slot_sizes(dims)
    rows = outs[0].shape[0] // sa
    came = []
    for rb in range(1, sb):
        came.append(hop(outs[rb], dims, n_head, 2, -rb))
    part = lambda array, ra: array[ra * rows : (ra + 1) * rows]
    line = []
    for ra in range(1, sa):
        total = add_all(part(outs[0], ra), [part(c, ra) for c in came], jnp.bfloat16)
        line.append(hop(total, dims, n_head, 1, -ra))
    total = add_all(part(outs[0], 0), [part(c, 0) for c in came] + line, jnp.bfloat16)
    if r0 == 0:
        return total
    return hop(total, dims, n_head, 0, -r0)


def slot_source(key, dims):
    place = lax.axis_index("ctx")
    core = lax.axis_index("head") % 2
    orders = phase_dims(dims)
    sources = []
    for order in orders:
        coords = [place // (dims[1] * dims[2]), place // dims[2] % dims[1], place % dims[2]]
        for dim, by in zip(order, key, strict=True):
            coords[dim] = (coords[dim] - by) % dims[dim]
        sources.append((coords[0] * dims[1] + coords[1]) * dims[2] + coords[2])
    return jnp.where(core == 0, sources[0], sources[1]).astype(jnp.int32)


def expert_body(n_a, n_b, n_expert, cap, n_tiles, src_ref, slot_ref, gate_ref, *refs):
    n_blocks = n_a * n_b
    blocks = refs[:n_blocks]
    gate_own, up_own, down_own, gate_oth, up_oth, down_oth = refs[n_blocks : n_blocks + 6]
    outs = refs[n_blocks + 6 : n_blocks + 6 + n_b]
    picked, hidden_of, scaled, select = refs[n_blocks + 6 + n_b :]
    expert = pl.program_id(0)
    tile = pl.program_id(1)
    tokens = blocks[0].shape[0]

    @pl.when((expert == 0) & (tile == 0))
    def _():
        for b in range(n_blocks):
            src = src_ref[b]
            for e in range(n_expert):
                wanted = slot_ref[src, pl.ds(e, 1), :]
                at = lax.broadcasted_iota(jnp.int32, (cap, tokens), 0)
                hit = (at == jnp.broadcast_to(wanted, (cap, tokens))).astype(jnp.float32)
                select[b, pl.ds(e * cap, cap), :] = hit.astype(jnp.bfloat16)
            got = jnp.dot(select[b], blocks[b][...], preferred_element_type=jnp.float32).astype(
                jnp.bfloat16
            )
            for e in range(n_expert):
                picked[e, pl.ds(b * cap, cap), :] = got[e * cap : (e + 1) * cap]

    def step(w_gate, w_up):
        tokens_in = picked[expert]
        gate_h = jnp.dot(tokens_in, w_gate[0], preferred_element_type=jnp.float32)
        up_h = jnp.dot(tokens_in, w_up[0], preferred_element_type=jnp.float32)
        hidden = gate_h * (1.0 / (1.0 + jnp.exp(-gate_h))) * up_h
        hidden_of[tile] = hidden.astype(jnp.bfloat16)

    def finish(w_down):
        hidden = jnp.concatenate([hidden_of[i] for i in range(n_tiles)], axis=1)
        result = jnp.dot(hidden, w_down[0], preferred_element_type=jnp.float32)
        for b in range(n_blocks):
            src = src_ref[b]
            weight_row = gate_ref[src, pl.ds(expert, 1), :]
            hit = select[b, pl.ds(expert * cap, cap), :].astype(jnp.float32)
            weight = jnp.sum(hit * weight_row, axis=1, keepdims=True)
            scaled[b, pl.ds(expert * cap, cap), :] = (
                result[b * cap : (b + 1) * cap] * weight
            ).astype(jnp.bfloat16)

    @pl.when(expert < n_expert // 2)
    def _():
        step(gate_own, up_own)

        @pl.when(tile == n_tiles - 1)
        def _():
            finish(down_own)

    @pl.when(expert >= n_expert // 2)
    def _():
        step(gate_oth, up_oth)

        @pl.when(tile == n_tiles - 1)
        def _():
            finish(down_oth)

    @pl.when((tile == n_tiles - 1) & (expert == n_expert - 1))
    def _():
        for b in range(n_blocks):
            back = jnp.transpose(select[b].astype(jnp.float32)).astype(jnp.bfloat16)
            outs[b // n_a][pl.ds(b % n_a * tokens, tokens), :] = jnp.dot(
                back, scaled[b], preferred_element_type=jnp.float32
            ).astype(jnp.bfloat16)


def run_experts(group, sources, slot_of, gate_of, own, other, cap):
    n_b, n_a = len(group), len(group[0])
    blocks = [block for line in group for block in line]
    n_blocks = len(blocks)
    tokens, width = blocks[0].shape
    per_dev, _, hidden = own[0].shape
    n_expert = 2 * per_dev
    tile_f = 256 if hidden % 256 == 0 else hidden
    n_tiles = hidden // tile_f
    last = n_tiles - 1
    whole = lambda shape: pl.BlockSpec(
        shape, lambda e, f, s: (0,) * len(shape), pipeline_mode=pl.Buffered(1)
    )

    def own_at(e, f):
        here = e < per_dev
        return jnp.where(here, e, per_dev - 1), jnp.where(here, f, last)

    def other_at(e, f):
        here = e >= per_dev
        return jnp.where(here, e - per_dev, 0), jnp.where(here, f, 0)

    def in_spec(at):
        return pl.BlockSpec((1, width, tile_f), lambda e, f, s: (at(e, f)[0], 0, at(e, f)[1]))

    def out_spec(at):
        return pl.BlockSpec((1, hidden, width), lambda e, f, s: (at(e, f)[0], 0, 0))

    rows = n_blocks * cap
    flops = 2 * n_expert * rows * width * hidden * 3
    moved = 2 * (2 * n_blocks * tokens * width + n_expert * 3 * width * hidden)
    return pl.pallas_call(
        functools.partial(expert_body, n_a, n_b, n_expert, cap, n_tiles),
        out_shape=[jax.ShapeDtypeStruct((n_a * tokens, width), jnp.bfloat16)] * n_b,
        grid_spec=pltpu.PrefetchScalarGridSpec(
            num_scalar_prefetch=1,
            grid=(n_expert, n_tiles),
            in_specs=[whole(slot_of.shape), whole(gate_of.shape)]
            + [whole((tokens, width))] * n_blocks
            + [in_spec(own_at), in_spec(own_at), out_spec(own_at)]
            + [in_spec(other_at), in_spec(other_at), out_spec(other_at)],
            out_specs=[whole((n_a * tokens, width))] * n_b,
            scratch_shapes=[
                pltpu.VMEM((n_expert, rows, width), jnp.bfloat16),
                pltpu.VMEM((n_tiles, rows, tile_f), jnp.bfloat16),
                pltpu.VMEM((n_blocks, n_expert * cap, width), jnp.bfloat16),
                pltpu.VMEM((n_blocks, n_expert * cap, tokens), jnp.bfloat16),
            ],
        ),
        compiler_params=pltpu.CompilerParams(
            dimension_semantics=("arbitrary", "arbitrary"), vmem_limit_bytes=60 * 1024 * 1024
        ),
        cost_estimate=pl.CostEstimate(
            flops=flops, bytes_accessed=moved, transcendentals=n_expert * rows * hidden
        ),
    )(sources, slot_of, gate_of, *blocks, *own, *other)


def two_terms(exact):
    high = exact.astype(jnp.bfloat16)
    return high, (exact - high.astype(jnp.float32)).astype(jnp.bfloat16)


def mm(lhs, rhs, at_lhs, at_rhs):
    return lax.dot_general(
        lhs, rhs, (((at_lhs,), (at_rhs,)), ((), ())), preferred_element_type=jnp.float32
    )


def mm_split(exact, narrow, at_lhs, at_rhs):
    high, low = two_terms(exact)
    return mm(high, narrow, at_lhs, at_rhs) + mm(low, narrow, at_lhs, at_rhs)


def unit_rows(vectors):
    floats = vectors.astype(jnp.float32)
    return floats * lax.rsqrt(jnp.sum(floats * floats, axis=-1, keepdims=True) + norm_eps)


def down_rows(row, lanes):
    return jnp.transpose(jnp.broadcast_to(row, (lanes, row.shape[1])))


def prep_body(rows, mine_ref, key_ref, value_ref, cumul_ref, unit_ref, *refs):
    heads, length, depth = key_ref.shape
    plane = heads * depth // rows
    gram_refs, held_refs = refs[:plane], refs[plane : 2 * plane]
    gram_all, held_all = refs[2 * plane :]
    last = cumul_ref[:, length - 1 : length]
    chunk = min(rows, depth)
    for h in range(heads):
        unit = unit_rows(key_ref[h]).astype(jnp.bfloat16)
        unit_ref[h] = unit
        left = last[h : h + 1] - cumul_ref[h : h + 1, :]
        faded = unit.astype(jnp.float32) * jnp.exp(down_rows(left, depth))
        high, low = two_terms(faded)
        gram = mm(high, unit, 0, 0) + mm(low, unit, 0, 0)
        held = mm(value_ref[h], high, 0, 0) + mm(value_ref[h], low, 0, 0)
        for start in range(0, depth, chunk):
            piece, at = divmod(h * depth + start, rows)
            gram_all[piece, at : at + chunk, :] = gram[start : start + chunk]
            held_all[piece, at : at + chunk, :] = held[start : start + chunk]
    tails = jnp.broadcast_to(last, (heads, depth))
    for k in range(plane):
        piece = mine_ref[0] ^ k
        gram_refs[k][0:rows, :] = gram_all[piece]
        gram_refs[k][rows : rows + heads, :] = tails
        held_refs[k][...] = held_all[piece].astype(jnp.bfloat16)


def prep(place, keys, values, cumul_log, plane):
    heads, length, depth = keys.shape
    rows = heads * depth // plane
    outs = (
        [jax.ShapeDtypeStruct(keys.shape, jnp.bfloat16)]
        + [jax.ShapeDtypeStruct((rows + heads, depth), jnp.float32)] * plane
        + [jax.ShapeDtypeStruct((rows, depth), jnp.bfloat16)] * plane
    )
    whole = lambda a: pl.BlockSpec(a.shape, lambda i, s: (0,) * len(a.shape))
    unit, *pieces = pl.pallas_call(
        functools.partial(prep_body, rows),
        out_shape=outs,
        grid_spec=pltpu.PrefetchScalarGridSpec(
            num_scalar_prefetch=1,
            grid=(1,),
            in_specs=[whole(keys), whole(values), whole(cumul_log)],
            out_specs=[whole(out) for out in outs],
            scratch_shapes=[pltpu.VMEM((plane, rows, depth), jnp.float32)] * 2,
        ),
        cost_estimate=pl.CostEstimate(
            flops=8 * heads * length * depth * depth,
            bytes_accessed=8 * heads * length * depth,
            transcendentals=heads * length * depth,
        ),
        name="prep",
    )(place, keys, values, cumul_log)
    return unit, pieces[:plane], pieces[plane:]


def plane_sums(tails, mine):
    count = len(tails)
    upto, before = [], []
    for k in range(count):
        total = jnp.zeros_like(tails[0])
        for j in range(count):
            total = total + jnp.where((mine ^ j) < (mine ^ k), tails[j], 0.0)
        before.append(total)
        upto.append(total + tails[k])
    return upto, before, functools.reduce(lambda x, y: x + y, tails)


def by_row(factors, table_ref, mine, rows, depth):
    table_ref[...] = factors
    span = max(1, rows // depth)
    first = mine * rows // depth
    return [table_ref[pl.ds(first + i, 1), :] for i in range(span)]


def weighted(factors, piece_ref, rows):
    step = rows // len(factors)
    return [
        f * piece_ref[i * step : (i + 1) * step, :].astype(jnp.float32)
        for i, f in enumerate(factors)
    ]


def mid_body(count, rows, tailed, mine_ref, *refs):
    pieces, tail_refs, up_ref, table_ref = refs[:count], refs[count : -2], refs[-2], refs[-1]
    heads, depth = table_ref.shape
    mine = mine_ref[0]
    tails = [t[...] for t in tail_refs]
    upto, _, every = plane_sums(tails, mine)
    total = None
    for k in range(count):
        factors = by_row(jnp.exp(every - upto[k]), table_ref, mine, rows, depth)
        term = weighted(factors, pieces[k], rows)
        total = term if total is None else [x + y for x, y in zip(total, term, strict=True)]
    step = rows // len(total)
    for i, part in enumerate(total):
        up_ref[i * step : (i + 1) * step, :] = part.astype(up_ref.dtype)
    if tailed:
        up_ref[rows : rows + heads, :] = every


def post_body(count, shifts, rows, mine_ref, *refs):
    pieces, tail_refs = refs[:count], refs[count : 2 * count]
    came = refs[2 * count : 2 * count + shifts]
    came_tails = refs[2 * count + shifts : 2 * count + 2 * shifts]
    outs, table_ref = refs[2 * count + 2 * shifts : -1], refs[-1]
    heads, depth = table_ref.shape
    mine = mine_ref[0]
    upto, before, _ = plane_sums([t[...] for t in tail_refs], mine)
    lost = jnp.zeros((heads, depth), jnp.float32)
    below = None
    for r in range(shifts):
        factors = by_row(jnp.exp(lost), table_ref, mine, rows, depth)
        term = weighted(factors, came[r], rows)
        below = term if below is None else [x + y for x, y in zip(below, term, strict=True)]
        lost = lost + came_tails[r][...]
    for k in range(count):
        factors = by_row(jnp.exp(before[k]), table_ref, mine, rows, depth)
        if below is None:
            total = [jnp.zeros((rows // len(factors), depth), jnp.float32)] * len(factors)
        else:
            total = [f * part for f, part in zip(factors, below, strict=True)]
        for j in range(count):
            if j == k:
                continue
            earlier = (mine ^ j) < (mine ^ k)
            share = jnp.where(earlier, jnp.exp(jnp.where(earlier, before[k] - upto[j], 0.0)), 0.0)
            factors = by_row(share, table_ref, mine, rows, depth)
            term = weighted(factors, pieces[j], rows)
            total = [x + y for x, y in zip(total, term, strict=True)]
        step = rows // len(total)
        for i, part in enumerate(total):
            outs[k][i * step : (i + 1) * step, :] = part.astype(outs[k].dtype)


def state_call(body, mine, arrays, blocks, outs, heads, depth):
    fixed = lambda block: pl.BlockSpec(block[0], lambda i, s: block[1])
    return pl.pallas_call(
        body,
        out_shape=outs,
        grid_spec=pltpu.PrefetchScalarGridSpec(
            num_scalar_prefetch=1,
            grid=(1,),
            in_specs=[fixed(block) for block in blocks],
            out_specs=[fixed((out.shape, (0, 0))) for out in outs],
            scratch_shapes=[pltpu.VMEM((heads, depth), jnp.float32)],
        ),
        cost_estimate=pl.CostEstimate(
            flops=2**21, bytes_accessed=2**21, transcendentals=2**12
        ),
    )(mine, *arrays)


def plane_pairs(n_ctx, plane, k):
    return [(i, i // plane * plane + (i % plane ^ k)) for i in range(n_ctx)]


def up_pairs(n_ctx, plane, r):
    return [(i, i + r * plane) for i in range(n_ctx) if i + r * plane < n_ctx]


class Exchange:
    def __init__(self, dims, rows, heads, depth):
        self.dims, self.rows, self.heads, self.depth = dims, rows, heads, depth
        self.plane = dims[1] * dims[2]
        self.n_ctx = dims[0] * self.plane
        self.mine = lax.rem(lax.axis_index("ctx"), self.plane).astype(jnp.int32)
        self.place = self.mine.reshape(1)
        self.whole = ((rows, depth), (0, 0))
        self.tail = ((heads, depth), (rows // heads, 0))

    def send_in(self, pieces):
        got = []
        for k in range(self.plane):
            piece = pieces[k]
            if k:
                piece = lax.ppermute(piece, "ctx", plane_pairs(self.n_ctx, self.plane, k))
            got.append(piece)
        return got

    def totals(self, got, tailed):
        own_tails = got is tailed
        size = self.rows + (self.heads if own_tails else 0)
        out = jax.ShapeDtypeStruct((size, self.depth), got[0].dtype)
        return state_call(
            functools.partial(mid_body, self.plane, self.rows, own_tails),
            self.place,
            [*got, *tailed],
            [self.whole] * self.plane + [self.tail] * self.plane,
            [out],
            self.heads,
            self.depth,
        )[0]

    def send_up(self, up):
        came = []
        for r in range(1, self.dims[0]):
            came.append(lax.ppermute(up, "ctx", up_pairs(self.n_ctx, self.plane, r)))
        return came

    def priors(self, got, tailed, came, came_tailed):
        shifts = self.dims[0] - 1
        out = jax.ShapeDtypeStruct((self.rows, self.depth), got[0].dtype)
        return state_call(
            functools.partial(post_body, self.plane, shifts, self.rows),
            self.place,
            [*got, *tailed, *came, *came_tailed],
            [self.whole] * self.plane
            + [self.tail] * self.plane
            + [self.whole] * shifts
            + [self.tail] * shifts,
            [out] * self.plane,
            self.heads,
            self.depth,
        )

    def send_out(self, priors):
        result = [priors[0]]
        for k in range(1, self.plane):
            result.append(lax.ppermute(priors[k], "ctx", plane_pairs(self.n_ctx, self.plane, k)))
        return result


def causal(cumul):
    length = cumul.shape[1]
    at = lax.broadcasted_iota(jnp.int32, (length, length), 0)
    of = lax.broadcasted_iota(jnp.int32, (length, length), 1)
    gap = down_rows(cumul, length) - jnp.broadcast_to(cumul, (length, length))
    return jnp.where(at >= of, jnp.exp(jnp.where(at >= of, gap, 0.0)), 0.0)


def prior_of(head, piece_refs, mine, depth):
    rows = piece_refs[0].shape[0]
    chunk = min(rows, depth)
    parts = []
    for start in range(0, depth, chunk):
        first = head * depth + start
        piece = first // rows
        at = pl.multiple_of(first % rows, chunk)
        part = jnp.zeros((chunk, depth), jnp.float32)
        for k, ref in enumerate(piece_refs):
            part = jnp.where((piece ^ mine) == k, ref[pl.ds(at, chunk), :].astype(jnp.float32), part)
        parts.append(part)
    return parts[0] if len(parts) == 1 else jnp.concatenate(parts, axis=0)


def solve_body(per_step, mine_ref, query_ref, unit_ref, cumul_ref, ridge_ref, *refs):
    pieces, answer_ref = refs[:-1], refs[-1]
    mine = mine_ref[0]
    length, depth = query_ref.shape[1:]
    spans = range(per_step)
    heads = [pl.program_id(0) * per_step + i for i in spans]
    units = [unit_ref[i] for i in spans]
    shares = [causal(cumul_ref[i]) for i in spans]
    starts = [jnp.exp(down_rows(cumul_ref[i], depth)) for i in spans]
    grams = [two_terms(prior_of(h, pieces, mine, depth)) for h in heads]
    remain = [unit_rows(query_ref[i]) for i in spans]
    direction = list(remain)
    answer = [jnp.zeros((length, depth), jnp.float32) for _ in spans]
    norm_now = [jnp.sum(r * r, axis=-1, keepdims=True) for r in remain]
    for _ in range(CG_STEPS):
        for i in spans:
            high, low = two_terms(direction[i])
            scores = (mm(high, units[i], 1, 1) + mm(low, units[i], 1, 1)) * shares[i]
            g_high, g_low = grams[i]
            prior = mm(high, g_high, 1, 1) + mm(low, g_high, 1, 1) + mm(high, g_low, 1, 1)
            applied = (
                starts[i] * prior
                + mm_split(scores, units[i], 1, 0)
                + ridge_ref[i] * direction[i]
            )
            length_of = norm_now[i] / jnp.sum(direction[i] * applied, axis=-1, keepdims=True)
            answer[i] = answer[i] + length_of * direction[i]
            remain[i] = remain[i] - length_of * applied
            norm_next = jnp.sum(remain[i] * remain[i], axis=-1, keepdims=True)
            direction[i] = remain[i] + (norm_next / norm_now[i]) * direction[i]
            norm_now[i] = norm_next
    for i in spans:
        answer_ref[i] = answer[i]


def read_body(per_step, mine_ref, answer_ref, unit_ref, value_ref, cumul_ref, *refs):
    pieces, out_ref = refs[:-1], refs[-1]
    mine = mine_ref[0]
    depth = answer_ref.shape[2]
    for i in range(per_step):
        head = pl.program_id(0) * per_step + i
        high, low = two_terms(answer_ref[i])
        held = prior_of(head, pieces, mine, depth).astype(jnp.bfloat16)
        start = jnp.exp(down_rows(cumul_ref[i], depth))
        prior = start * (mm(high, held, 1, 1) + mm(low, held, 1, 1))
        scores = (mm(high, unit_ref[i], 1, 1) + mm(low, unit_ref[i], 1, 1)) * causal(cumul_ref[i])
        out = prior + mm_split(scores, value_ref[i], 1, 0)
        out_ref[:, i * depth : (i + 1) * depth] = out.astype(jnp.bfloat16)


def head_call(body, mine, arrays, pieces, out, per_step, flops):
    heads, length, depth = arrays[0].shape
    by_head = lambda a: pl.BlockSpec((per_step, *a.shape[1:]), lambda i, s: (i, 0, 0))
    if len(out.shape) == 3:
        out_spec = by_head(out)
    else:
        out_spec = pl.BlockSpec((length, per_step * depth), lambda i, s: (0, i))
    return pl.pallas_call(
        functools.partial(body, per_step),
        out_shape=out,
        grid_spec=pltpu.PrefetchScalarGridSpec(
            num_scalar_prefetch=1,
            grid=(heads // per_step,),
            in_specs=[by_head(a) for a in arrays]
            + [pl.BlockSpec(p.shape, lambda i, s: (0, 0)) for p in pieces],
            out_specs=out_spec,
        ),
        cost_estimate=pl.CostEstimate(
            flops=flops, bytes_accessed=12 * heads * length * depth, transcendentals=heads * length * length
        ),
    )(mine, *arrays, *pieces)


def on_device(
    queries,
    key_vecs,
    values,
    log_decay,
    ridge_diag,
    residual,
    w_out,
    norm_gain,
    routes,
    gate_probs,
    w_gate,
    w_up,
    w_down,
):
    tok_dev, heads_dev, head_dim = queries.shape
    n_ctx = lax.axis_size("ctx")
    n_head = lax.axis_size("head")
    dims = grid_dims(n_ctx)
    core = lax.axis_index("head")
    swap = [(i, i ^ 1) for i in range(n_head)]

    tok_moe, top_count = routes.shape
    per_dev = w_gate.shape[0]
    expert_total = per_dev * n_ctx * n_head
    cap = 2 * tok_moe * top_count // expert_total
    own = (w_gate, w_up, w_down)
    other = tuple(lax.ppermute(w, "head", swap) for w in own)
    named = routes[:, :, None] == jnp.arange(expert_total, dtype=jnp.int32)[None, None, :]
    dense = jnp.sum(jnp.where(named, gate_probs[:, :, None], 0.0), axis=1)
    table = dense.T.reshape(n_ctx, n_head * per_dev, tok_moe)
    keys_h = key_vecs.transpose(1, 0, 2)
    values_h = values.transpose(1, 0, 2)
    queries_h = queries.transpose(1, 0, 2)
    cumul_log = jnp.cumsum(log_decay, axis=1)
    cumul_h = cumul_log[:, None, :]
    plane = dims[1] * dims[2]
    swap_state = Exchange(dims, heads_dev * head_dim // plane, heads_dev, head_dim)
    unit_h, gram_pieces, held_pieces = prep(swap_state.place, keys_h, values_h, cumul_log, plane)
    gram_got = swap_state.send_in(gram_pieces)
    held_got = swap_state.send_in(held_pieces)
    gram_up = swap_state.totals(gram_got, gram_got)
    gram_came = swap_state.send_up(gram_up)
    held_up = swap_state.totals(held_got, gram_got)
    held_came = swap_state.send_up(held_up)
    gram_prior = swap_state.priors(gram_got, gram_got, gram_came, gram_came)
    gram_prior = swap_state.send_out(gram_prior)
    held_prior = swap_state.priors(held_got, gram_got, held_came, gram_came)
    held_prior = swap_state.send_out(held_prior)
    per_step = 4 if heads_dev % 4 == 0 else 1
    work = heads_dev * tok_dev * head_dim
    answer = head_call(
        solve_body,
        swap_state.place,
        [queries_h, unit_h, cumul_h, ridge_diag[:, None, :]],
        gram_prior,
        jax.ShapeDtypeStruct(queries_h.shape, jnp.float32),
        per_step,
        CG_STEPS * work * (8 * tok_dev + 6 * head_dim),
    )
    mesa_rows = head_call(
        read_body,
        swap_state.place,
        [answer, unit_h, values_h, cumul_h],
        held_prior,
        jax.ShapeDtypeStruct((tok_dev, heads_dev * head_dim), jnp.bfloat16),
        per_step,
        work * (8 * tok_dev + 4 * head_dim),
    )
    partial = jnp.dot(mesa_rows, w_out, preferred_element_type=jnp.float32)
    sent = lax.dynamic_slice_in_dim(partial, (1 - core) * tok_moe, tok_moe, 0)
    came = lax.ppermute(sent.astype(jnp.bfloat16), "head", swap)
    kept = lax.dynamic_slice_in_dim(partial, core * tok_moe, tok_moe, 0)
    attended = (residual.astype(jnp.float32) + kept + came.astype(jnp.float32)).astype(jnp.bfloat16)
    att_f = attended.astype(jnp.float32)
    normed = (
        att_f * lax.rsqrt(jnp.mean(att_f * att_f, axis=-1, keepdims=True) + norm_eps) * norm_gain
    ).astype(jnp.bfloat16)

    groups = spread(normed, dims, n_head)
    gate_of = lax.all_to_all(table, "ctx", split_axis=0, concat_axis=0, tiled=True)
    split = gate_of.reshape(n_ctx, n_head, per_dev, tok_moe)
    gate_of = jnp.where(core == 0, split, split[:, ::-1]).reshape(gate_of.shape)
    routed = (gate_of != 0.0).astype(jnp.bfloat16)
    earlier = (jnp.arange(tok_moe)[:, None] < jnp.arange(tok_moe)[None, :]).astype(jnp.bfloat16)
    before = jnp.einsum("set,tu->seu", routed, earlier, preferred_element_type=jnp.float32)
    slot_of = jnp.where(gate_of != 0.0, before.astype(jnp.int32), -1)

    back = []
    for r0, group in groups.items():
        sources = [
            slot_source((r0, ra, rb), dims) for rb in range(len(group)) for ra in range(len(group[0]))
        ]
        sources = lax.optimization_barrier(jnp.stack(sources))
        outs = run_experts(group, sources, slot_of, gate_of, own, other, cap)
        back.append(collect(outs, r0, dims, n_head))
    layer_out = add_all(att_f, back, jnp.bfloat16)
    return (attended, layer_out)


def solution(mesh):
    in_specs = (
        P("ctx", "head", None),
        P("ctx", "head", None),
        P("ctx", "head", None),
        P("head", "ctx"),
        P("head", None),
        P(("ctx", "head"), None),
        P("head", None),
        P(),
        P(("ctx", "head"), None),
        P(("ctx", "head"), None),
        P(("ctx", "head"), None, None),
        P(("ctx", "head"), None, None),
        P(("ctx", "head"), None, None),
    )
    out_specs = (P(("ctx", "head"), None), P(("ctx", "head"), None))

    return jax.shard_map(
        on_device, mesh=mesh, in_specs=in_specs, out_specs=out_specs, check_vma=False
    )
```

profile of v0, /device:TPU:0, one launch (start us, length us, event | category | flops | bytes accessed | tf_op | source)
XLA Modules:
  0.0 315.6 jit_solution(15852400832614401275)
XLA Ops:
  2.8 2.4 copy_bitcast_fusion
  5.2 4.0 %prep.1 = (bf16[8,256,128]{2,1,0:T(8,128)(2,1)}, f32[264,128]{1,0:T(8,128)}, f32[264,128]{1,0:T(8,128)}, f32[264,128]{1,0:T(8,128)}, f32[264,128]{1,0:T(8,128)},...) custom-call(s32[1]{0:T(128)} %bitcast.mine_ref, ...), custom_call_target="tpu_custom_call" | custom-call | flops 268435456 | bytes 2097152 | tf_op jit(solution)/shard_map/prep/pallas_call | solution.py:299
  9.1 3.0 collective-permute-start
  16.4 3.0 collective-permute-done.1.refs_2_.refs_6_
  23.2 3.5 %collective-permute-start.3 = (f32[264,128]{1,0:T(8,128)}, f32[264,128]{1,0:T(8,128)S(1)}, u32[]{:S(2)}, u32[]{:S(2)}) collective-permute-start(f32[264,128]{1,0:T(8,128)} %shard_map.140), channel_id=1, source_target_pairs={{0,8},{2,10},{4,12},{6,14},{8,16},{10,18},{12,20},{14,22},{16,24},... | collective-permute-start | bytes 405512 | tf_op jit(solution)/shard_map/ppermute | solution.py:460
  26.7 4.5 %collective-permute-start.4 = (f32[264,128]{1,0:T(8,128)}, f32[264,128]{1,0:T(8,128)S(1)}, u32[]{:S(2)}, u32[]{:S(2)}) collective-permute-start(f32[264,128]{1,0:T(8,128)} %shard_map.140), channel_id=1, source_target_pairs={{0,16},{2,18},{4,20},{6,22},{8,24},{10,26},{12,28},{14,30},{1,17},... | collective-permute-start | bytes 405512 | tf_op jit(solution)/shard_map/ppermute | solution.py:460
  46.8 2.2 shard_map.141
  61.5 12.0 %shard_map.142.answer_ref = f32[8,256,128]{2,1,0:T(8,128)} custom-call(s32[1]{0:T(128)} %bitcast.mine_ref, bf16[8,256,128]{2,1,0:T(8,128)(2,1)} %bitcast.37, bf16[8,256,128]{2,1,0:T(8,128)(2,1)} %get-tuple-element.27.unit_ref, f32[8,1,256]{2,1,0:T(1,128)} %bitcast.38, f32[8,1,128]{2,1,0:T(1,128)} %bitcast.41, f32[256,128]{1,0:T(8,128)} %get-tuple-element.32.refs_0_, ...), custom_call_target="tpu_custom_call" | custom-call | flops 2952790016 | bytes 3145728 | tf_op jit(solution)/shard_map/pallas_call | solution.py:566
  74.2 5.0 %shard_map.145 = bf16[256,1024]{1,0:T(8,128)(2,1)} custom-call(s32[1]{0:T(128)} %bitcast.mine_ref, f32[8,256,128]{2,1,0:T(8,128)} %shard_map.142.answer_ref, bf16[8,256,128]{2,1,0:T(8,128)(2,1)} %get-tuple-element.27.unit_ref, bf16[8,256,128]{2,1,0:T(8,128)(2,1)} %get-tuple-element.56.value_ref, f32[8,1,256]{2,1,0:T(1,128)} %bitcast.39, ...), custom_call_target="tpu_custom_call" | custom-call | flops 671088640 | bytes 3145728 | tf_op jit(solution)/shard_map/pallas_call | solution.py:566
  79.2 3.7 %fusion.12 = f32[256,2048]{1,0:T(8,128)S(1)} fusion(bf16[256,1024]{1,0:T(8,128)(2,1)} %shard_map.145, bf16[1024,2048]{1,0:T(8,128)(2,1)} %param.19), kind=kOutput, calls=%fused_computation.40 | convolution fusion | flops 1073741824 | bytes 6815744 | tf_op jit(solution)/shard_map/dot_general | solution.py:651
  91.0 23.3 %collective-permute-done.41.refs_0_ = bf16[128,2048]{1,0:T(8,128)(2,1)} collective-permute-done((bf16[128,2048]{1,0:T(8,128)(2,1)S(1)}, bf16[128,2048]{1,0:T(8,128)(2,1)}, u32[]{:S(2)}, u32[]{:S(2)}) %collective-permute-start.41) | collective-permute-done | bytes 524320 | tf_op jit(solution)/shard_map/ppermute | solution.py:45
  115.3 23.3 %collective-permute-done.27.refs_0_ = bf16[128,2048]{1,0:T(8,128)(2,1)} collective-permute-done((bf16[128,2048]{1,0:T(8,128)(2,1)S(1)}, bf16[128,2048]{1,0:T(8,128)(2,1)}, u32[]{:S(2)}, u32[]{:S(2)}) %collective-permute-start.27) | collective-permute-done | bytes 524320 | tf_op jit(solution)/shard_map/ppermute | solution.py:45
  141.6 3.7 %all-to-all-start = ((f32[16,2,128]{2,1,0:T(2,128)}), f32[16,2,128]{2,1,0:T(2,128)S(1)}, u32[]{:S(2)}, u32[]{:S(2)}) async-start(f32[16,2,128]{2,1,0:T(2,128)} %bitcast.13), calls=%async_computation | async-start | bytes 32768 | tf_op jit(solution)/shard_map/all_to_all | solution.py:662
  147.3 6.1 %collective-permute-done.43.refs_2_ = bf16[128,2048]{1,0:T(8,128)(2,1)} collective-permute-done((bf16[128,2048]{1,0:T(8,128)(2,1)}, bf16[128,2048]{1,0:T(8,128)(2,1)}, u32[]{:S(2)}, u32[]{:S(2)}) %collective-permute-start.43) | collective-permute-done | bytes 524320 | tf_op jit(solution)/shard_map/ppermute | solution.py:45
  157.0 10.3 %collective-permute-done.28.refs_1_ = bf16[128,2048]{1,0:T(8,128)(2,1)} collective-permute-done((bf16[128,2048]{1,0:T(8,128)(2,1)}, bf16[128,2048]{1,0:T(8,128)(2,1)}, u32[]{:S(2)}, u32[]{:S(2)}) %collective-permute-start.28) | collective-permute-done | bytes 524320 | tf_op jit(solution)/shard_map/ppermute | solution.py:45
  173.5 17.0 %shard_map.149 = (bf16[256,2048]{1,0:T(8,128)(2,1)}, bf16[256,2048]{1,0:T(8,128)(2,1)}) custom-call(s32[4]{0:T(128)} %pad_add_fusion.3.src_ref, s32[16,2,128]{2,1,0:T(2,128)} %fusion.10.slot_ref, f32[16,2,128]{2,1,0:T(2,128)} %get-tuple-element.55.gate_ref, bf16[128,2048]{1,0:T(8,128)(2,1)} %collective-permute-done.41.refs_0_, ...), custom_call_target="tpu_custom_call" | custom-call | flops 4831838208 | bytes 23068672 | tf_op jit(solution)/shard_map/pallas_call | solution.py:211
  193.4 16.8 %shard_map.148 = (bf16[256,2048]{1,0:T(8,128)(2,1)}, bf16[256,2048]{1,0:T(8,128)(2,1)}) custom-call(s32[4]{0:T(128)} %pad_add_fusion.2.src_ref, s32[16,2,128]{2,1,0:T(2,128)} %fusion.10.slot_ref, f32[16,2,128]{2,1,0:T(2,128)} %get-tuple-element.55.gate_ref, bf16[128,2048]{1,0:T(8,128)(2,1)} %collective-permute-done.34.refs_0_, ...), custom_call_target="tpu_custom_call" | custom-call | flops 4831838208 | bytes 23068672 | tf_op jit(solution)/shard_map/pallas_call | solution.py:211
  212.3 17.1 %shard_map.147 = (bf16[256,2048]{1,0:T(8,128)(2,1)}, bf16[256,2048]{1,0:T(8,128)(2,1)}) custom-call(s32[4]{0:T(128)} %pad_add_fusion.1.src_ref, s32[16,2,128]{2,1,0:T(2,128)} %fusion.10.slot_ref, f32[16,2,128]{2,1,0:T(2,128)} %get-tuple-element.55.gate_ref, bf16[128,2048]{1,0:T(8,128)(2,1)} %collective-permute-done.27.refs_0_, ...), custom_call_target="tpu_custom_call" | custom-call | flops 4831838208 | bytes 23068672 | tf_op jit(solution)/shard_map/pallas_call | solution.py:211
  231.1 16.9 %shard_map.146 = (bf16[256,2048]{1,0:T(8,128)(2,1)}, bf16[256,2048]{1,0:T(8,128)(2,1)}) custom-call(s32[4]{0:T(128)} %pad_add_fusion.src_ref, s32[16,2,128]{2,1,0:T(2,128)} %fusion.10.slot_ref, f32[16,2,128]{2,1,0:T(2,128)} %get-tuple-element.55.gate_ref, bf16[128,2048]{1,0:T(8,128)(2,1)} %copy-done.6, bf16[128,2048]{1,0:T(8,128)(2,1)} %copy-done.16, ...), custom_call_target="tpu_custom_call" | custom-call | flops 4831838208 | bytes 23068672 | tf_op jit(solution)/shard_map/pallas_call | solution.py:211
  255.8 18.4 %collective-permute-done.25 = bf16[256,2048]{1,0:T(8,128)(2,1)S(1)} collective-permute-done((bf16[256,2048]{1,0:T(8,128)(2,1)}, bf16[256,2048]{1,0:T(8,128)(2,1)S(1)}, u32[]{:S(2)}, u32[]{:S(2)}) %collective-permute-start.25) | collective-permute-done | bytes 1048608 | tf_op jit(solution)/shard_map/ppermute | solution.py:45
  278.4 3.9 %collective-permute-start.40 = (bf16[128,2048]{1,0:T(8,128)(2,1)S(1)}, bf16[128,2048]{1,0:T(8,128)(2,1)S(1)}, u32[]{:S(2)}, u32[]{:S(2)}) collective-permute-start(bf16[128,2048]{1,0:T(8,128)(2,1)S(1)} %add_convert_fusion.2), channel_id=1, source_target_pairs={{0,24},{1,25},{2,26},{3,27},{4,28},{5,29},{6,30},{7,31},{8,0},{9,1... | collective-permute-start | bytes 1572872 | tf_op jit(solution)/shard_map/ppermute | solution.py:45
  283.7 8.2 %collective-permute-done.47 = bf16[128,2048]{1,0:T(8,128)(2,1)S(1)} collective-permute-done((bf16[128,2048]{1,0:T(8,128)(2,1)S(1)}, bf16[128,2048]{1,0:T(8,128)(2,1)S(1)}, u32[]{:S(2)}, u32[]{:S(2)}) %collective-permute-start.47) | collective-permute-done | bytes 524320 | tf_op jit(solution)/shard_map/ppermute | solution.py:45
  291.9 3.2 %collective-permute-done.40 = bf16[128,2048]{1,0:T(8,128)(2,1)S(1)} collective-permute-done((bf16[128,2048]{1,0:T(8,128)(2,1)S(1)}, bf16[128,2048]{1,0:T(8,128)(2,1)S(1)}, u32[]{:S(2)}, u32[]{:S(2)}) %collective-permute-start.40) | collective-permute-done | bytes 524320 | tf_op jit(solution)/shard_map/ppermute | solution.py:45
  295.1 19.1 %collective-permute-done.33 = bf16[128,2048]{1,0:T(8,128)(2,1)S(1)} collective-permute-done((bf16[128,2048]{1,0:T(8,128)(2,1)S(1)}, bf16[128,2048]{1,0:T(8,128)(2,1)S(1)}, u32[]{:S(2)}, u32[]{:S(2)}) %collective-permute-start.33) | collective-permute-done | bytes 524320 | tf_op jit(solution)/shard_map/ppermute | solution.py:45
  (190 shorter events, 83.7 us)
Async XLA Ops:
  13.6 20.0 %collective-permute-start.9 = (bf16[256,128]{1,0:T(8,128)(2,1)}, bf16[256,128]{1,0:T(8,128)(2,1)S(1)}, u32[]{:S(2)}, u32[]{:S(2)}) collective-permute-start(bf16[256,128]{1,0:T(8,128)(2,1)} %get-tuple-element.37), channel_id=1, source_target_pairs={{0,2},{2,0},{4,6},{6,4},{8,10},{10,8},{12,14},{14,12},{16,18},{18,... | collective-permute-start | bytes 196616 | tf_op jit(solution)/shard_map/ppermute | solution.py:439
  23.2 20.7 %collective-permute-start.3 = (f32[264,128]{1,0:T(8,128)}, f32[264,128]{1,0:T(8,128)S(1)}, u32[]{:S(2)}, u32[]{:S(2)}) collective-permute-start(f32[264,128]{1,0:T(8,128)} %shard_map.140), channel_id=1, source_target_pairs={{0,8},{2,10},{4,12},{6,14},{8,16},{10,18},{12,20},{14,22},{16,24},... | collective-permute-start | bytes 405512 | tf_op jit(solution)/shard_map/ppermute | solution.py:460
  83.9 85.3 %collective-permute-start.22 = (bf16[1,2048,768]{2,1,0:T(8,128)(2,1)S(1)}, bf16[1,2048,768]{2,1,0:T(8,128)(2,1)}, u32[]{:S(2)}, u32[]{:S(2)}) collective-permute-start(bf16[1,2048,768]{2,1,0:T(8,128)(2,1)S(1)} %copy-done), channel_id=1, source_target_pairs={{0,1},{1,0},{2,3},{3,2},{4,5},{5,4},{6,7},{7,6},{8,9},{9,8},{10,11... | collective-permute-start | bytes 9437192 | tf_op jit(solution)/shard_map/ppermute | solution.py:609
  84.4 87.0 %collective-permute-start.23 = (bf16[1,2048,768]{2,1,0:T(8,128)(2,1)}, bf16[1,2048,768]{2,1,0:T(8,128)(2,1)}, u32[]{:S(2)}, u32[]{:S(2)}) collective-permute-start(bf16[1,2048,768]{2,1,0:T(8,128)(2,1)} %refs_5_.7), channel_id=1, source_target_pairs={{0,1},{1,0},{2,3},{3,2},{4,5},{5,4},{6,7},{7,6},{8,9},{9,8},{10,11... | collective-permute-start | bytes 9437192 | tf_op jit(solution)/shard_map/ppermute | solution.py:609
  84.4 87.4 %collective-permute-start.24 = (bf16[1,768,2048]{2,1,0:T(8,128)(2,1)}, bf16[1,768,2048]{2,1,0:T(8,128)(2,1)}, u32[]{:S(2)}, u32[]{:S(2)}) collective-permute-start(bf16[1,768,2048]{2,1,0:T(8,128)(2,1)} %refs_6_.7), channel_id=1, source_target_pairs={{0,1},{1,0},{2,3},{3,2},{4,5},{5,4},{6,7},{7,6},{8,9},{9,8},{10,11... | collective-permute-start | bytes 9437192 | tf_op jit(solution)/shard_map/ppermute | solution.py:609
  89.0 25.4 %collective-permute-start.41 = (bf16[128,2048]{1,0:T(8,128)(2,1)S(1)}, bf16[128,2048]{1,0:T(8,128)(2,1)}, u32[]{:S(2)}, u32[]{:S(2)}) collective-permute-start(bf16[128,2048]{1,0:T(8,128)(2,1)S(1)} %fusion.2.refs_0_), channel_id=1, source_target_pairs={{0,24},{1,25},{2,26},{3,27},{4,28},{5,29},{6,30},{7,31},{8,0},{9,1... | collective-permute-start | bytes 1572872 | tf_op jit(solution)/shard_map/ppermute | solution.py:45
  89.0 25.3 %collective-permute-start.34 = (bf16[128,2048]{1,0:T(8,128)(2,1)S(1)}, bf16[128,2048]{1,0:T(8,128)(2,1)}, u32[]{:S(2)}, u32[]{:S(2)}) collective-permute-start(bf16[128,2048]{1,0:T(8,128)(2,1)S(1)} %fusion.2.refs_0_), channel_id=1, source_target_pairs={{0,8},{1,9},{2,10},{3,11},{4,12},{5,13},{6,14},{7,15},{8,16},{9,17... | collective-permute-start | bytes 1572872 | tf_op jit(solution)/shard_map/ppermute | solution.py:45
  114.3 24.2 %collective-permute-start.27 = (bf16[128,2048]{1,0:T(8,128)(2,1)S(1)}, bf16[128,2048]{1,0:T(8,128)(2,1)}, u32[]{:S(2)}, u32[]{:S(2)}) collective-permute-start(bf16[128,2048]{1,0:T(8,128)(2,1)S(1)} %fusion.2.refs_0_), channel_id=1, source_target_pairs={{0,16},{1,17},{2,18},{3,19},{4,20},{5,21},{6,22},{7,23},{8,24},{9,... | collective-permute-start | bytes 1572872 | tf_op jit(solution)/shard_map/ppermute | solution.py:45
  114.3 25.2 %collective-permute-start.42 = (bf16[128,2048]{1,0:T(8,128)(2,1)}, bf16[128,2048]{1,0:T(8,128)(2,1)}, u32[]{:S(2)}, u32[]{:S(2)}) collective-permute-start(bf16[128,2048]{1,0:T(8,128)(2,1)} %collective-permute-done.41.refs_0_), channel_id=1, source_target_pairs={{0,2},{1,5},{2,0},{3,7},{4,6},{5,1},{6,4},{7,3},{8,10},{9,13},{10,... | collective-permute-start | bytes 1572872 | tf_op jit(solution)/shard_map/ppermute | solution.py:45
  167.3 23.1 %collective-permute-start.19 = (bf16[128,2048]{1,0:T(8,128)(2,1)}, bf16[128,2048]{1,0:T(8,128)(2,1)S(1)}, u32[]{:S(2)}, u32[]{:S(2)}) collective-permute-start(bf16[128,2048]{1,0:T(8,128)(2,1)} %copy-done.6), channel_id=1, source_target_pairs={{0,2},{1,5},{2,0},{3,7},{4,6},{5,1},{6,4},{7,3},{8,10},{9,13},{10,... | collective-permute-start | bytes 1572872 | tf_op jit(solution)/shard_map/ppermute | solution.py:45
  168.8 22.1 %collective-permute-start.36 = (bf16[128,2048]{1,0:T(8,128)(2,1)}, bf16[128,2048]{1,0:T(8,128)(2,1)}, u32[]{:S(2)}, u32[]{:S(2)}) collective-permute-start(bf16[128,2048]{1,0:T(8,128)(2,1)} %collective-permute-done.34.refs_0_), channel_id=1, source_target_pairs={{0,4},{1,3},{2,6},{3,1},{4,0},{5,7},{6,2},{7,5},{8,12},{9,11},{10,... | collective-permute-start | bytes 1572872 | tf_op jit(solution)/shard_map/ppermute | solution.py:45
  169.2 23.4 %collective-permute-start.37 = (bf16[128,2048]{1,0:T(8,128)(2,1)}, bf16[128,2048]{1,0:T(8,128)(2,1)S(1)}, u32[]{:S(2)}, u32[]{:S(2)}) collective-permute-start(bf16[128,2048]{1,0:T(8,128)(2,1)} %collective-permute-done.35.refs_1_), channel_id=1, source_target_pairs={{0,4},{1,3},{2,6},{3,1},{4,0},{5,7},{6,2},{7,5},{8,12},{9,11},{10,... | collective-permute-start | bytes 1572872 | tf_op jit(solution)/shard_map/ppermute | solution.py:45
  171.4 38.7 %collective-permute-start.29 = (bf16[128,2048]{1,0:T(8,128)(2,1)}, bf16[128,2048]{1,0:T(8,128)(2,1)S(1)}, u32[]{:S(2)}, u32[]{:S(2)}) collective-permute-start(bf16[128,2048]{1,0:T(8,128)(2,1)} %collective-permute-done.27.refs_0_), channel_id=1, source_target_pairs={{0,4},{1,3},{2,6},{3,1},{4,0},{5,7},{6,2},{7,5},{8,12},{9,11},{10,... | collective-permute-start | bytes 1572872 | tf_op jit(solution)/shard_map/ppermute | solution.py:45
  171.8 39.7 %collective-permute-start.30 = (bf16[128,2048]{1,0:T(8,128)(2,1)}, bf16[128,2048]{1,0:T(8,128)(2,1)S(1)}, u32[]{:S(2)}, u32[]{:S(2)}) collective-permute-start(bf16[128,2048]{1,0:T(8,128)(2,1)} %collective-permute-done.28.refs_1_), channel_id=1, source_target_pairs={{0,4},{1,3},{2,6},{3,1},{4,0},{5,7},{6,2},{7,5},{8,12},{9,11},{10,... | collective-permute-start | bytes 1572872 | tf_op jit(solution)/shard_map/ppermute | solution.py:45
  190.5 39.8 %collective-permute-start.20 = (bf16[128,2048]{1,0:T(8,128)(2,1)S(1)}, bf16[128,2048]{1,0:T(8,128)(2,1)S(1)}, u32[]{:S(2)}, u32[]{:S(2)}) collective-permute-start(bf16[128,2048]{1,0:T(8,128)(2,1)S(1)} %copy-done.7), channel_id=1, source_target_pairs={{0,4},{1,3},{2,6},{3,1},{4,0},{5,7},{6,2},{7,5},{8,12},{9,11},{10,... | collective-permute-start | bytes 1572872 | tf_op jit(solution)/shard_map/ppermute | solution.py:45
  190.9 39.4 %collective-permute-start.21 = (bf16[128,2048]{1,0:T(8,128)(2,1)S(1)}, bf16[128,2048]{1,0:T(8,128)(2,1)}, u32[]{:S(2)}, u32[]{:S(2)}) collective-permute-start(bf16[128,2048]{1,0:T(8,128)(2,1)S(1)} %collective-permute-done.19.refs_1_), channel_id=1, source_target_pairs={{0,4},{1,3},{2,6},{3,1},{4,0},{5,7},{6,2},{7,5},{8,12},{9,11},{10,... | collective-permute-start | bytes 1572872 | tf_op jit(solution)/shard_map/ppermute | solution.py:45
  192.6 56.7 %collective-permute-start.45 = (bf16[256,2048]{1,0:T(8,128)(2,1)}, bf16[256,2048]{1,0:T(8,128)(2,1)}, u32[]{:S(2)}, u32[]{:S(2)}) collective-permute-start(bf16[256,2048]{1,0:T(8,128)(2,1)} %get-tuple-element.51), channel_id=1, source_target_pairs={{0,4},{1,3},{2,6},{3,1},{4,0},{5,7},{6,2},{7,5},{8,12},{9,11},{10,... | collective-permute-start | bytes 3145736 | tf_op jit(solution)/shard_map/ppermute | solution.py:45
  210.2 41.1 %collective-permute-start.38 = (bf16[256,2048]{1,0:T(8,128)(2,1)}, bf16[256,2048]{1,0:T(8,128)(2,1)}, u32[]{:S(2)}, u32[]{:S(2)}) collective-permute-start(bf16[256,2048]{1,0:T(8,128)(2,1)} %get-tuple-element.49), channel_id=1, source_target_pairs={{0,4},{1,3},{2,6},{3,1},{4,0},{5,7},{6,2},{7,5},{8,12},{9,11},{10,... | collective-permute-start | bytes 3145736 | tf_op jit(solution)/shard_map/ppermute | solution.py:45
  229.4 24.4 %collective-permute-start.31 = (bf16[256,2048]{1,0:T(8,128)(2,1)}, bf16[256,2048]{1,0:T(8,128)(2,1)}, u32[]{:S(2)}, u32[]{:S(2)}) collective-permute-start(bf16[256,2048]{1,0:T(8,128)(2,1)} %get-tuple-element.47), channel_id=1, source_target_pairs={{0,4},{1,3},{2,6},{3,1},{4,0},{5,7},{6,2},{7,5},{8,12},{9,11},{10,... | collective-permute-start | bytes 3145736 | tf_op jit(solution)/shard_map/ppermute | solution.py:45
  248.0 26.3 %collective-permute-start.25 = (bf16[256,2048]{1,0:T(8,128)(2,1)}, bf16[256,2048]{1,0:T(8,128)(2,1)S(1)}, u32[]{:S(2)}, u32[]{:S(2)}) collective-permute-start(bf16[256,2048]{1,0:T(8,128)(2,1)} %get-tuple-element.45), channel_id=1, source_target_pairs={{0,4},{1,3},{2,6},{3,1},{4,0},{5,7},{6,2},{7,5},{8,12},{9,11},{10,... | collective-permute-start | bytes 3145736 | tf_op jit(solution)/shard_map/ppermute | solution.py:45
  250.5 25.3 %collective-permute-start.46 = (bf16[128,2048]{1,0:T(8,128)(2,1)S(1)}, bf16[128,2048]{1,0:T(8,128)(2,1)S(1)}, u32[]{:S(2)}, u32[]{:S(2)}) collective-permute-start(bf16[128,2048]{1,0:T(8,128)(2,1)S(1)} %add_convert_fusion.1), channel_id=1, source_target_pairs={{0,2},{1,5},{2,0},{3,7},{4,6},{5,1},{6,4},{7,3},{8,10},{9,13},{10,... | collective-permute-start | bytes 1572872 | tf_op jit(solution)/shard_map/ppermute | solution.py:45
  252.5 24.6 %collective-permute-start.39 = (bf16[128,2048]{1,0:T(8,128)(2,1)S(1)}, bf16[128,2048]{1,0:T(8,128)(2,1)S(1)}, u32[]{:S(2)}, u32[]{:S(2)}) collective-permute-start(bf16[128,2048]{1,0:T(8,128)(2,1)S(1)} %add_convert_fusion.3), channel_id=1, source_target_pairs={{0,2},{1,5},{2,0},{3,7},{4,6},{5,1},{6,4},{7,3},{8,10},{9,13},{10,... | collective-permute-start | bytes 1572872 | tf_op jit(solution)/shard_map/ppermute | solution.py:45
  255.0 27.3 %collective-permute-start.32 = (bf16[128,2048]{1,0:T(8,128)(2,1)S(1)}, bf16[128,2048]{1,0:T(8,128)(2,1)S(1)}, u32[]{:S(2)}, u32[]{:S(2)}) collective-permute-start(bf16[128,2048]{1,0:T(8,128)(2,1)S(1)} %add_convert_fusion.5), channel_id=1, source_target_pairs={{0,2},{1,5},{2,0},{3,7},{4,6},{5,1},{6,4},{7,3},{8,10},{9,13},{10,... | collective-permute-start | bytes 1572872 | tf_op jit(solution)/shard_map/ppermute | solution.py:45
  283.5 30.7 %collective-permute-start.33 = (bf16[128,2048]{1,0:T(8,128)(2,1)S(1)}, bf16[128,2048]{1,0:T(8,128)(2,1)S(1)}, u32[]{:S(2)}, u32[]{:S(2)}) collective-permute-start(bf16[128,2048]{1,0:T(8,128)(2,1)S(1)} %add_convert_fusion.4), channel_id=1, source_target_pairs={{0,16},{1,17},{2,18},{3,19},{4,20},{5,21},{6,22},{7,23},{8,24},{9,... | collective-permute-start | bytes 1572872 | tf_op jit(solution)/shard_map/ppermute | solution.py:45
  (62 other events, 671.7 us)
where the time goes:
time: 317 us; the launch traced here: 316 us
  waiting for transfers between devices  122 us (38%)
  Pallas kernels  96.4 us (30%)
  starting transfers between devices  61.7 us (19%)
  other arithmetic  17.2 us (5%)
  local copies, waits for them, and re-layouts  13 us (4%)
  matrix products  3.88 us (1%)
    ppermute x26, waiting for transfers between devices, hop(): return lax.ppermute(block, BOTH, pairs)  112 us
    pallas_call x4, Pallas kernels, run_experts(): pl.pallas_call(functools.partial(expert_body, n_a, n_b, n_expert, cap, n_...  67.8 us
    ppermute x26, starting transfers between devices, hop(): return lax.ppermute(block, BOTH, pairs)  27.2 us
    pallas_call x2, Pallas kernels, head_call(): pl.pallas_call(functools.partial(body, per_step), out_shape=out, grid_spe...  17 us
    ppermute x6, starting transfers between devices, send_up(): came.append(lax.ppermute(up, 'ctx', up_pairs(self.n_ctx, self.plane, r)))  13.3 us
    ppermute x6, starting transfers between devices, send_in(): piece = lax.ppermute(piece, 'ctx', plane_pairs(self.n_ctx, self.plane, k))  9.43 us
    unnamed x75, local copies, waits for them, and re-layouts  8.96 us
    convert_element_type x8, other arithmetic, add_all(): return total.astype(dtype)  8.85 us
  transfers between devices with their start and end apart: 49, of which 15 were waited for; matrix products, arithmetic and copies ran while one was open for 5% of the time, Pallas kernels for 28%

commit v1 on v0

--- a/solution.py
+++ b/solution.py
@@ -62,13 +62,15 @@
             line.append(hop(head, dims, n_head, 1, ra))
         group = [line]
         for rb in range(1, sb):
-            group.append([hop(one, dims, n_head, 2, rb) for one in line])
+            sent = [hop(head, dims, n_head, 2, rb)]
+            sent += [hop(one, dims, n_head, 2, rb) for one in line[1:]]
+            group.append(sent)
         groups[r0] = group
     return groups
 
 
 def visit(size):
-    return [0] + sorted(range(1, size), key=lambda r: (-min(r, size - r), r))
+    return list(range(size))
 
 
 def add_all(first, others, dtype):

time: 317 us -> 312 us (0.984); the launches traced: 316 us -> 307 us
  waiting for transfers between devices: 122 us -> 90.6 us
  starting transfers between devices: 61.7 us -> 85.3 us
    ppermute x26, waiting for transfers between devices: 112 us -> 80.4 us  [hop(): return lax.ppermute(block, BOTH, pairs)]
    ppermute x26, starting transfers between devices: 27.2 us -> 50.8 us  [hop(): return lax.ppermute(block, BOTH, pairs)]
  transfers between devices with their start and end apart: 49 -> 49, of which waited for: 15 -> 16; matrix products, arithmetic and copies ran while one was open for 5% -> 5% of each run, Pallas kernels for 28% -> 28%
where the time goes in v1:
time: 312 us; the launch traced here: 307 us
  Pallas kernels  96.4 us (31%)
  waiting for transfers between devices  90.6 us (29%)
  starting transfers between devices  85.3 us (27%)
  other arithmetic  17.2 us (6%)
  local copies, waits for them, and re-layouts  12.6 us (4%)
  matrix products  3.88 us (1%)
    ppermute x26, waiting for transfers between devices, hop(): return lax.ppermute(block, BOTH, pairs)  80.4 us
    pallas_call x4, Pallas kernels, run_experts(): pl.pallas_call(functools.partial(expert_body, n_a, n_b, n_expert, cap, n_...  67.7 us
    ppermute x26, starting transfers between devices, hop(): return lax.ppermute(block, BOTH, pairs)  50.8 us
    pallas_call x2, Pallas kernels, head_call(): pl.pallas_call(functools.partial(body, per_step), out_shape=out, grid_spe...  17 us
    ppermute x6, starting transfers between devices, send_up(): came.append(lax.ppermute(up, 'ctx', up_pairs(self.n_ctx, self.plane, r)))  13.3 us
    ppermute x6, starting transfers between devices, send_in(): piece = lax.ppermute(piece, 'ctx', plane_pairs(self.n_ctx, self.plane, k))  9.43 us
    convert_element_type x8, other arithmetic, add_all(): return total.astype(dtype)  8.85 us
    ppermute x6, waiting for transfers between devices, send_in(): piece = lax.ppermute(piece, 'ctx', plane_pairs(self.n_ctx, self.plane, k))  8.69 us
  transfers between devices with their start and end apart: 49, of which 16 were waited for; matrix products, arithmetic and copies ran while one was open for 5% of the time, Pallas kernels for 28%

profile of v1, /device:TPU:0, one launch (start us, length us, event | category | flops | bytes accessed | tf_op | source)
XLA Modules:
  0.0 307.3 jit_solution(10247742431402566489)
XLA Ops:
  2.8 2.4 copy_bitcast_fusion
  5.2 4.0 %prep.1 = (bf16[8,256,128]{2,1,0:T(8,128)(2,1)}, f32[264,128]{1,0:T(8,128)}, f32[264,128]{1,0:T(8,128)}, f32[264,128]{1,0:T(8,128)}, f32[264,128]{1,0:T(8,128)},...) custom-call(s32[1]{0:T(128)} %bitcast.mine_ref, ...), custom_call_target="tpu_custom_call" | custom-call | flops 268435456 | bytes 2097152 | tf_op jit(solution)/shard_map/prep/pallas_call | solution.py:301
  9.1 3.0 collective-permute-start
  16.4 3.0 collective-permute-done.1.refs_2_.refs_6_
  23.2 3.5 %collective-permute-start.3 = (f32[264,128]{1,0:T(8,128)}, f32[264,128]{1,0:T(8,128)S(1)}, u32[]{:S(2)}, u32[]{:S(2)}) collective-permute-start(f32[264,128]{1,0:T(8,128)} %shard_map.140), channel_id=1, source_target_pairs={{0,8},{2,10},{4,12},{6,14},{8,16},{10,18},{12,20},{14,22},{16,24},... | collective-permute-start | bytes 405512 | tf_op jit(solution)/shard_map/ppermute | solution.py:462
  26.7 4.5 %collective-permute-start.4 = (f32[264,128]{1,0:T(8,128)}, f32[264,128]{1,0:T(8,128)S(1)}, u32[]{:S(2)}, u32[]{:S(2)}) collective-permute-start(f32[264,128]{1,0:T(8,128)} %shard_map.140), channel_id=1, source_target_pairs={{0,16},{2,18},{4,20},{6,22},{8,24},{10,26},{12,28},{14,30},{1,17},... | collective-permute-start | bytes 405512 | tf_op jit(solution)/shard_map/ppermute | solution.py:462
  61.5 12.0 %shard_map.142.answer_ref = f32[8,256,128]{2,1,0:T(8,128)} custom-call(s32[1]{0:T(128)} %bitcast.mine_ref, bf16[8,256,128]{2,1,0:T(8,128)(2,1)} %bitcast.37, bf16[8,256,128]{2,1,0:T(8,128)(2,1)} %get-tuple-element.27.unit_ref, f32[8,1,256]{2,1,0:T(1,128)} %bitcast.38, f32[8,1,128]{2,1,0:T(1,128)} %bitcast.41, f32[256,128]{1,0:T(8,128)} %get-tuple-element.32.refs_0_, ...), custom_call_target="tpu_custom_call" | custom-call | flops 2952790016 | bytes 3145728 | tf_op jit(solution)/shard_map/pallas_call | solution.py:568
  74.2 5.0 %shard_map.145 = bf16[256,1024]{1,0:T(8,128)(2,1)} custom-call(s32[1]{0:T(128)} %bitcast.mine_ref, f32[8,256,128]{2,1,0:T(8,128)} %shard_map.142.answer_ref, bf16[8,256,128]{2,1,0:T(8,128)(2,1)} %get-tuple-element.27.unit_ref, bf16[8,256,128]{2,1,0:T(8,128)(2,1)} %get-tuple-element.56.value_ref, f32[8,1,256]{2,1,0:T(1,128)} %bitcast.39, ...), custom_call_target="tpu_custom_call" | custom-call | flops 671088640 | bytes 3145728 | tf_op jit(solution)/shard_map/pallas_call | solution.py:568
  79.2 3.7 %fusion.12 = f32[256,2048]{1,0:T(8,128)S(1)} fusion(bf16[256,1024]{1,0:T(8,128)(2,1)} %shard_map.145, bf16[1024,2048]{1,0:T(8,128)(2,1)} %param.19), kind=kOutput, calls=%fused_computation.40 | convolution fusion | flops 1073741824 | bytes 6815744 | tf_op jit(solution)/shard_map/dot_general | solution.py:653
  89.8 13.5 %collective-permute-done.41.refs_0_ = bf16[128,2048]{1,0:T(8,128)(2,1)} collective-permute-done((bf16[128,2048]{1,0:T(8,128)(2,1)S(1)}, bf16[128,2048]{1,0:T(8,128)(2,1)}, u32[]{:S(2)}, u32[]{:S(2)}) %collective-permute-start.41) | collective-permute-done | bytes 524320 | tf_op jit(solution)/shard_map/ppermute | solution.py:45
  103.3 22.4 %collective-permute-start.27 = (bf16[128,2048]{1,0:T(8,128)(2,1)S(1)}, bf16[128,2048]{1,0:T(8,128)(2,1)}, u32[]{:S(2)}, u32[]{:S(2)}) collective-permute-start(bf16[128,2048]{1,0:T(8,128)(2,1)S(1)} %fusion.2.refs_0_), channel_id=1, source_target_pairs={{0,8},{1,9},{2,10},{3,11},{4,12},{5,13},{6,14},{7,15},{8,16},{9,17... | collective-permute-start | bytes 1572872 | tf_op jit(solution)/shard_map/ppermute | solution.py:45
  125.7 9.8 %collective-permute-done.34.refs_0_ = bf16[128,2048]{1,0:T(8,128)(2,1)} collective-permute-done((bf16[128,2048]{1,0:T(8,128)(2,1)S(1)}, bf16[128,2048]{1,0:T(8,128)(2,1)}, u32[]{:S(2)}, u32[]{:S(2)}) %collective-permute-start.34) | collective-permute-done | bytes 524320 | tf_op jit(solution)/shard_map/ppermute | solution.py:45
  137.9 11.7 %collective-permute-done.42.refs_1_ = bf16[128,2048]{1,0:T(8,128)(2,1)} collective-permute-done((bf16[128,2048]{1,0:T(8,128)(2,1)}, bf16[128,2048]{1,0:T(8,128)(2,1)}, u32[]{:S(2)}, u32[]{:S(2)}) %collective-permute-start.42) | collective-permute-done | bytes 524320 | tf_op jit(solution)/shard_map/ppermute | solution.py:45
  151.7 3.7 %all-to-all-start = ((f32[16,2,128]{2,1,0:T(2,128)}), f32[16,2,128]{2,1,0:T(2,128)S(1)}, u32[]{:S(2)}, u32[]{:S(2)}) async-start(f32[16,2,128]{2,1,0:T(2,128)} %bitcast.13), calls=%async_computation | async-start | bytes 32768 | tf_op jit(solution)/shard_map/all_to_all | solution.py:664
  163.3 7.2 %collective-permute-done.28.refs_1_ = bf16[128,2048]{1,0:T(8,128)(2,1)} collective-permute-done((bf16[128,2048]{1,0:T(8,128)(2,1)}, bf16[128,2048]{1,0:T(8,128)(2,1)}, u32[]{:S(2)}, u32[]{:S(2)}) %collective-permute-start.28) | collective-permute-done | bytes 524320 | tf_op jit(solution)/shard_map/ppermute | solution.py:45
  171.9 3.1 %collective-permute-done.44.refs_3_ = bf16[128,2048]{1,0:T(8,128)(2,1)} collective-permute-done((bf16[128,2048]{1,0:T(8,128)(2,1)}, bf16[128,2048]{1,0:T(8,128)(2,1)}, u32[]{:S(2)}, u32[]{:S(2)}) %collective-permute-start.44) | collective-permute-done | bytes 524320 | tf_op jit(solution)/shard_map/ppermute | solution.py:45
  179.8 17.0 %shard_map.149 = (bf16[256,2048]{1,0:T(8,128)(2,1)}, bf16[256,2048]{1,0:T(8,128)(2,1)}) custom-call(s32[4]{0:T(128)} %pad_add_fusion.3.src_ref, s32[16,2,128]{2,1,0:T(2,128)} %fusion.10.slot_ref, f32[16,2,128]{2,1,0:T(2,128)} %get-tuple-element.55.gate_ref, bf16[128,2048]{1,0:T(8,128)(2,1)} %collective-permute-done.41.refs_0_, ...), custom_call_target="tpu_custom_call" | custom-call | flops 4831838208 | bytes 23068672 | tf_op jit(solution)/shard_map/pallas_call | solution.py:213
  199.7 16.8 %shard_map.148 = (bf16[256,2048]{1,0:T(8,128)(2,1)}, bf16[256,2048]{1,0:T(8,128)(2,1)}) custom-call(s32[4]{0:T(128)} %pad_add_fusion.2.src_ref, s32[16,2,128]{2,1,0:T(2,128)} %fusion.10.slot_ref, f32[16,2,128]{2,1,0:T(2,128)} %get-tuple-element.55.gate_ref, bf16[128,2048]{1,0:T(8,128)(2,1)} %collective-permute-done.34.refs_0_, ...), custom_call_target="tpu_custom_call" | custom-call | flops 4831838208 | bytes 23068672 | tf_op jit(solution)/shard_map/pallas_call | solution.py:213
  218.6 17.1 %shard_map.147 = (bf16[256,2048]{1,0:T(8,128)(2,1)}, bf16[256,2048]{1,0:T(8,128)(2,1)}) custom-call(s32[4]{0:T(128)} %pad_add_fusion.1.src_ref, s32[16,2,128]{2,1,0:T(2,128)} %fusion.10.slot_ref, f32[16,2,128]{2,1,0:T(2,128)} %get-tuple-element.55.gate_ref, bf16[128,2048]{1,0:T(8,128)(2,1)} %collective-permute-done.27.refs_0_, ...), custom_call_target="tpu_custom_call" | custom-call | flops 4831838208 | bytes 23068672 | tf_op jit(solution)/shard_map/pallas_call | solution.py:213
  237.4 16.9 %shard_map.146 = (bf16[256,2048]{1,0:T(8,128)(2,1)}, bf16[256,2048]{1,0:T(8,128)(2,1)}) custom-call(s32[4]{0:T(128)} %pad_add_fusion.src_ref, s32[16,2,128]{2,1,0:T(2,128)} %fusion.10.slot_ref, f32[16,2,128]{2,1,0:T(2,128)} %get-tuple-element.55.gate_ref, bf16[128,2048]{1,0:T(8,128)(2,1)} %copy-done.6, bf16[128,2048]{1,0:T(8,128)(2,1)} %copy-done.16, ...), custom_call_target="tpu_custom_call" | custom-call | flops 4831838208 | bytes 23068672 | tf_op jit(solution)/shard_map/pallas_call | solution.py:213
  262.9 17.7 %collective-permute-done.25 = bf16[256,2048]{1,0:T(8,128)(2,1)S(1)} collective-permute-done((bf16[256,2048]{1,0:T(8,128)(2,1)}, bf16[256,2048]{1,0:T(8,128)(2,1)S(1)}, u32[]{:S(2)}, u32[]{:S(2)}) %collective-permute-start.25) | collective-permute-done | bytes 1048608 | tf_op jit(solution)/shard_map/ppermute | solution.py:45
  287.0 3.2 %collective-permute-start.33 = (bf16[128,2048]{1,0:T(8,128)(2,1)S(1)}, bf16[128,2048]{1,0:T(8,128)(2,1)S(1)}, u32[]{:S(2)}, u32[]{:S(2)}) collective-permute-start(bf16[128,2048]{1,0:T(8,128)(2,1)S(1)} %add_convert_fusion.4), channel_id=1, source_target_pairs={{0,24},{1,25},{2,26},{3,27},{4,28},{5,29},{6,30},{7,31},{8,0},{9,1... | collective-permute-start | bytes 1572872 | tf_op jit(solution)/shard_map/ppermute | solution.py:45
  290.2 4.6 %collective-permute-done.47 = bf16[128,2048]{1,0:T(8,128)(2,1)S(1)} collective-permute-done((bf16[128,2048]{1,0:T(8,128)(2,1)S(1)}, bf16[128,2048]{1,0:T(8,128)(2,1)S(1)}, u32[]{:S(2)}, u32[]{:S(2)}) %collective-permute-start.47) | collective-permute-done | bytes 524320 | tf_op jit(solution)/shard_map/ppermute | solution.py:45
  294.9 11.1 %collective-permute-done.40 = bf16[128,2048]{1,0:T(8,128)(2,1)S(1)} collective-permute-done((bf16[128,2048]{1,0:T(8,128)(2,1)S(1)}, bf16[128,2048]{1,0:T(8,128)(2,1)S(1)}, u32[]{:S(2)}, u32[]{:S(2)}) %collective-permute-start.40) | collective-permute-done | bytes 524320 | tf_op jit(solution)/shard_map/ppermute | solution.py:45
  (190 shorter events, 89.0 us)
Async XLA Ops:
  13.6 20.0 %collective-permute-start.9 = (bf16[256,128]{1,0:T(8,128)(2,1)}, bf16[256,128]{1,0:T(8,128)(2,1)S(1)}, u32[]{:S(2)}, u32[]{:S(2)}) collective-permute-start(bf16[256,128]{1,0:T(8,128)(2,1)} %get-tuple-element.37), channel_id=1, source_target_pairs={{0,2},{2,0},{4,6},{6,4},{8,10},{10,8},{12,14},{14,12},{16,18},{18,... | collective-permute-start | bytes 196616 | tf_op jit(solution)/shard_map/ppermute | solution.py:441
  23.2 20.7 %collective-permute-start.3 = (f32[264,128]{1,0:T(8,128)}, f32[264,128]{1,0:T(8,128)S(1)}, u32[]{:S(2)}, u32[]{:S(2)}) collective-permute-start(f32[264,128]{1,0:T(8,128)} %shard_map.140), channel_id=1, source_target_pairs={{0,8},{2,10},{4,12},{6,14},{8,16},{10,18},{12,20},{14,22},{16,24},... | collective-permute-start | bytes 405512 | tf_op jit(solution)/shard_map/ppermute | solution.py:462
  83.9 92.1 %collective-permute-start.22 = (bf16[1,2048,768]{2,1,0:T(8,128)(2,1)S(1)}, bf16[1,2048,768]{2,1,0:T(8,128)(2,1)}, u32[]{:S(2)}, u32[]{:S(2)}) collective-permute-start(bf16[1,2048,768]{2,1,0:T(8,128)(2,1)S(1)} %copy-done), channel_id=1, source_target_pairs={{0,1},{1,0},{2,3},{3,2},{4,5},{5,4},{6,7},{7,6},{8,9},{9,8},{10,11... | collective-permute-start | bytes 9437192 | tf_op jit(solution)/shard_map/ppermute | solution.py:611
  84.4 93.3 %collective-permute-start.23 = (bf16[1,2048,768]{2,1,0:T(8,128)(2,1)}, bf16[1,2048,768]{2,1,0:T(8,128)(2,1)}, u32[]{:S(2)}, u32[]{:S(2)}) collective-permute-start(bf16[1,2048,768]{2,1,0:T(8,128)(2,1)} %refs_5_.7), channel_id=1, source_target_pairs={{0,1},{1,0},{2,3},{3,2},{4,5},{5,4},{6,7},{7,6},{8,9},{9,8},{10,11... | collective-permute-start | bytes 9437192 | tf_op jit(solution)/shard_map/ppermute | solution.py:611
  84.4 94.1 %collective-permute-start.24 = (bf16[1,768,2048]{2,1,0:T(8,128)(2,1)}, bf16[1,768,2048]{2,1,0:T(8,128)(2,1)}, u32[]{:S(2)}, u32[]{:S(2)}) collective-permute-start(bf16[1,768,2048]{2,1,0:T(8,128)(2,1)} %refs_6_.7), channel_id=1, source_target_pairs={{0,1},{1,0},{2,3},{3,2},{4,5},{5,4},{6,7},{7,6},{8,9},{9,8},{10,11... | collective-permute-start | bytes 9437192 | tf_op jit(solution)/shard_map/ppermute | solution.py:611
  89.0 46.5 %collective-permute-start.34 = (bf16[128,2048]{1,0:T(8,128)(2,1)S(1)}, bf16[128,2048]{1,0:T(8,128)(2,1)}, u32[]{:S(2)}, u32[]{:S(2)}) collective-permute-start(bf16[128,2048]{1,0:T(8,128)(2,1)S(1)} %fusion.2.refs_0_), channel_id=1, source_target_pairs={{0,16},{1,17},{2,18},{3,19},{4,20},{5,21},{6,22},{7,23},{8,24},{9,... | collective-permute-start | bytes 1572872 | tf_op jit(solution)/shard_map/ppermute | solution.py:45
  103.3 33.1 %collective-permute-start.27 = (bf16[128,2048]{1,0:T(8,128)(2,1)S(1)}, bf16[128,2048]{1,0:T(8,128)(2,1)}, u32[]{:S(2)}, u32[]{:S(2)}) collective-permute-start(bf16[128,2048]{1,0:T(8,128)(2,1)S(1)} %fusion.2.refs_0_), channel_id=1, source_target_pairs={{0,8},{1,9},{2,10},{3,11},{4,12},{5,13},{6,14},{7,15},{8,16},{9,17... | collective-permute-start | bytes 1572872 | tf_op jit(solution)/shard_map/ppermute | solution.py:45
  136.4 21.1 %collective-permute-start.43 = (bf16[128,2048]{1,0:T(8,128)(2,1)}, bf16[128,2048]{1,0:T(8,128)(2,1)}, u32[]{:S(2)}, u32[]{:S(2)}) collective-permute-start(bf16[128,2048]{1,0:T(8,128)(2,1)} %collective-permute-done.41.refs_0_), channel_id=1, source_target_pairs={{0,4},{1,3},{2,6},{3,1},{4,0},{5,7},{6,2},{7,5},{8,12},{9,11},{10,... | collective-permute-start | bytes 1572872 | tf_op jit(solution)/shard_map/ppermute | solution.py:45
  170.5 26.2 %collective-permute-start.19 = (bf16[128,2048]{1,0:T(8,128)(2,1)}, bf16[128,2048]{1,0:T(8,128)(2,1)S(1)}, u32[]{:S(2)}, u32[]{:S(2)}) collective-permute-start(bf16[128,2048]{1,0:T(8,128)(2,1)} %copy-done.6), channel_id=1, source_target_pairs={{0,2},{1,5},{2,0},{3,7},{4,6},{5,1},{6,4},{7,3},{8,10},{9,13},{10,... | collective-permute-start | bytes 1572872 | tf_op jit(solution)/shard_map/ppermute | solution.py:45
  175.1 22.6 %collective-permute-start.36 = (bf16[128,2048]{1,0:T(8,128)(2,1)}, bf16[128,2048]{1,0:T(8,128)(2,1)}, u32[]{:S(2)}, u32[]{:S(2)}) collective-permute-start(bf16[128,2048]{1,0:T(8,128)(2,1)} %collective-permute-done.34.refs_0_), channel_id=1, source_target_pairs={{0,4},{1,3},{2,6},{3,1},{4,0},{5,7},{6,2},{7,5},{8,12},{9,11},{10,... | collective-permute-start | bytes 1572872 | tf_op jit(solution)/shard_map/ppermute | solution.py:45
  175.9 22.9 %collective-permute-start.37 = (bf16[128,2048]{1,0:T(8,128)(2,1)}, bf16[128,2048]{1,0:T(8,128)(2,1)S(1)}, u32[]{:S(2)}, u32[]{:S(2)}) collective-permute-start(bf16[128,2048]{1,0:T(8,128)(2,1)} %collective-permute-done.35.refs_1_), channel_id=1, source_target_pairs={{0,4},{1,3},{2,6},{3,1},{4,0},{5,7},{6,2},{7,5},{8,12},{9,11},{10,... | collective-permute-start | bytes 1572872 | tf_op jit(solution)/shard_map/ppermute | solution.py:45
  177.7 38.8 %collective-permute-start.29 = (bf16[128,2048]{1,0:T(8,128)(2,1)}, bf16[128,2048]{1,0:T(8,128)(2,1)S(1)}, u32[]{:S(2)}, u32[]{:S(2)}) collective-permute-start(bf16[128,2048]{1,0:T(8,128)(2,1)} %collective-permute-done.27.refs_0_), channel_id=1, source_target_pairs={{0,4},{1,3},{2,6},{3,1},{4,0},{5,7},{6,2},{7,5},{8,12},{9,11},{10,... | collective-permute-start | bytes 1572872 | tf_op jit(solution)/shard_map/ppermute | solution.py:45
  178.6 39.2 %collective-permute-start.30 = (bf16[128,2048]{1,0:T(8,128)(2,1)}, bf16[128,2048]{1,0:T(8,128)(2,1)S(1)}, u32[]{:S(2)}, u32[]{:S(2)}) collective-permute-start(bf16[128,2048]{1,0:T(8,128)(2,1)} %collective-permute-done.28.refs_1_), channel_id=1, source_target_pairs={{0,4},{1,3},{2,6},{3,1},{4,0},{5,7},{6,2},{7,5},{8,12},{9,11},{10,... | collective-permute-start | bytes 1572872 | tf_op jit(solution)/shard_map/ppermute | solution.py:45
  196.7 39.9 %collective-permute-start.20 = (bf16[128,2048]{1,0:T(8,128)(2,1)S(1)}, bf16[128,2048]{1,0:T(8,128)(2,1)S(1)}, u32[]{:S(2)}, u32[]{:S(2)}) collective-permute-start(bf16[128,2048]{1,0:T(8,128)(2,1)S(1)} %copy-done.7), channel_id=1, source_target_pairs={{0,4},{1,3},{2,6},{3,1},{4,0},{5,7},{6,2},{7,5},{8,12},{9,11},{10,... | collective-permute-start | bytes 1572872 | tf_op jit(solution)/shard_map/ppermute | solution.py:45
  197.7 39.0 %collective-permute-start.21 = (bf16[128,2048]{1,0:T(8,128)(2,1)S(1)}, bf16[128,2048]{1,0:T(8,128)(2,1)}, u32[]{:S(2)}, u32[]{:S(2)}) collective-permute-start(bf16[128,2048]{1,0:T(8,128)(2,1)S(1)} %collective-permute-done.19.refs_1_), channel_id=1, source_target_pairs={{0,4},{1,3},{2,6},{3,1},{4,0},{5,7},{6,2},{7,5},{8,12},{9,11},{10,... | collective-permute-start | bytes 1572872 | tf_op jit(solution)/shard_map/ppermute | solution.py:45
  198.8 56.7 %collective-permute-start.45 = (bf16[256,2048]{1,0:T(8,128)(2,1)}, bf16[256,2048]{1,0:T(8,128)(2,1)}, u32[]{:S(2)}, u32[]{:S(2)}) collective-permute-start(bf16[256,2048]{1,0:T(8,128)(2,1)} %get-tuple-element.51), channel_id=1, source_target_pairs={{0,4},{1,3},{2,6},{3,1},{4,0},{5,7},{6,2},{7,5},{8,12},{9,11},{10,... | collective-permute-start | bytes 3145736 | tf_op jit(solution)/shard_map/ppermute | solution.py:45
  216.5 41.8 %collective-permute-start.38 = (bf16[256,2048]{1,0:T(8,128)(2,1)}, bf16[256,2048]{1,0:T(8,128)(2,1)}, u32[]{:S(2)}, u32[]{:S(2)}) collective-permute-start(bf16[256,2048]{1,0:T(8,128)(2,1)} %get-tuple-element.49), channel_id=1, source_target_pairs={{0,4},{1,3},{2,6},{3,1},{4,0},{5,7},{6,2},{7,5},{8,12},{9,11},{10,... | collective-permute-start | bytes 3145736 | tf_op jit(solution)/shard_map/ppermute | solution.py:45
  235.7 24.4 %collective-permute-start.31 = (bf16[256,2048]{1,0:T(8,128)(2,1)}, bf16[256,2048]{1,0:T(8,128)(2,1)}, u32[]{:S(2)}, u32[]{:S(2)}) collective-permute-start(bf16[256,2048]{1,0:T(8,128)(2,1)} %get-tuple-element.47), channel_id=1, source_target_pairs={{0,4},{1,3},{2,6},{3,1},{4,0},{5,7},{6,2},{7,5},{8,12},{9,11},{10,... | collective-permute-start | bytes 3145736 | tf_op jit(solution)/shard_map/ppermute | solution.py:45
  254.3 26.3 %collective-permute-start.25 = (bf16[256,2048]{1,0:T(8,128)(2,1)}, bf16[256,2048]{1,0:T(8,128)(2,1)S(1)}, u32[]{:S(2)}, u32[]{:S(2)}) collective-permute-start(bf16[256,2048]{1,0:T(8,128)(2,1)} %get-tuple-element.45), channel_id=1, source_target_pairs={{0,4},{1,3},{2,6},{3,1},{4,0},{5,7},{6,2},{7,5},{8,12},{9,11},{10,... | collective-permute-start | bytes 3145736 | tf_op jit(solution)/shard_map/ppermute | solution.py:45
  256.7 25.6 %collective-permute-start.46 = (bf16[128,2048]{1,0:T(8,128)(2,1)S(1)}, bf16[128,2048]{1,0:T(8,128)(2,1)S(1)}, u32[]{:S(2)}, u32[]{:S(2)}) collective-permute-start(bf16[128,2048]{1,0:T(8,128)(2,1)S(1)} %add_convert_fusion.1), channel_id=1, source_target_pairs={{0,2},{1,5},{2,0},{3,7},{4,6},{5,1},{6,4},{7,3},{8,10},{9,13},{10,... | collective-permute-start | bytes 1572872 | tf_op jit(solution)/shard_map/ppermute | solution.py:45
  259.6 24.1 %collective-permute-start.39 = (bf16[128,2048]{1,0:T(8,128)(2,1)S(1)}, bf16[128,2048]{1,0:T(8,128)(2,1)S(1)}, u32[]{:S(2)}, u32[]{:S(2)}) collective-permute-start(bf16[128,2048]{1,0:T(8,128)(2,1)S(1)} %add_convert_fusion.3), channel_id=1, source_target_pairs={{0,2},{1,5},{2,0},{3,7},{4,6},{5,1},{6,4},{7,3},{8,10},{9,13},{10,... | collective-permute-start | bytes 1572872 | tf_op jit(solution)/shard_map/ppermute | solution.py:45
  261.2 24.5 %collective-permute-start.32 = (bf16[128,2048]{1,0:T(8,128)(2,1)S(1)}, bf16[128,2048]{1,0:T(8,128)(2,1)S(1)}, u32[]{:S(2)}, u32[]{:S(2)}) collective-permute-start(bf16[128,2048]{1,0:T(8,128)(2,1)S(1)} %add_convert_fusion.5), channel_id=1, source_target_pairs={{0,2},{1,5},{2,0},{3,7},{4,6},{5,1},{6,4},{7,3},{8,10},{9,13},{10,... | collective-permute-start | bytes 1572872 | tf_op jit(solution)/shard_map/ppermute | solution.py:45
  285.0 20.9 %collective-permute-start.40 = (bf16[128,2048]{1,0:T(8,128)(2,1)S(1)}, bf16[128,2048]{1,0:T(8,128)(2,1)S(1)}, u32[]{:S(2)}, u32[]{:S(2)}) collective-permute-start(bf16[128,2048]{1,0:T(8,128)(2,1)S(1)} %add_convert_fusion.2), channel_id=1, source_target_pairs={{0,16},{1,17},{2,18},{3,19},{4,20},{5,21},{6,22},{7,23},{8,24},{9,... | collective-permute-start | bytes 1572872 | tf_op jit(solution)/shard_map/ppermute | solution.py:45
  287.0 18.9 %collective-permute-start.33 = (bf16[128,2048]{1,0:T(8,128)(2,1)S(1)}, bf16[128,2048]{1,0:T(8,128)(2,1)S(1)}, u32[]{:S(2)}, u32[]{:S(2)}) collective-permute-start(bf16[128,2048]{1,0:T(8,128)(2,1)S(1)} %add_convert_fusion.4), channel_id=1, source_target_pairs={{0,24},{1,25},{2,26},{3,27},{4,28},{5,29},{6,30},{7,31},{8,0},{9,1... | collective-permute-start | bytes 1572872 | tf_op jit(solution)/shard_map/ppermute | solution.py:45
  (62 other events, 652.1 us)

commit v2 on v1

--- a/solution.py
+++ b/solution.py
@@ -52,11 +52,12 @@
 
 def spread(block, dims, n_head):
     s0, sa, sb = slot_sizes(dims)
-    heads = [block]
-    for r0 in visit(s0)[1:]:
-        heads.append(hop(block, dims, n_head, 0, r0))
+    heads = {0: block}
+    for r0 in range(1, s0):
+        heads[r0] = hop(block, dims, n_head, 0, r0)
     groups = {}
-    for r0, head in zip(visit(s0), heads, strict=True):
+    for r0 in visit(s0):
+        head = heads[r0]
         line = [head]
         for ra in range(1, sa):
             line.append(hop(head, dims, n_head, 1, ra))
@@ -70,7 +71,7 @@
 
 
 def visit(size):
-    return list(range(size))
+    return [*range(1, size), 0]
 
 
 def add_all(first, others, dtype):

time: 312 us -> 312 us (level)
  no operation moved by 1% of the time
where the time goes in v2:
time: 312 us; the launch traced here: 307 us
  Pallas kernels  96.4 us (31%)
  waiting for transfers between devices  90.6 us (29%)
  starting transfers between devices  85.3 us (27%)
  other arithmetic  17.2 us (6%)
  local copies, waits for them, and re-layouts  12.6 us (4%)
  matrix products  3.88 us (1%)
    ppermute x26, waiting for transfers between devices, hop(): return lax.ppermute(block, BOTH, pairs)  80.4 us
    pallas_call x4, Pallas kernels, run_experts(): pl.pallas_call(functools.partial(expert_body, n_a, n_b, n_expert, cap, n_...  67.7 us
    ppermute x26, starting transfers between devices, hop(): return lax.ppermute(block, BOTH, pairs)  50.8 us
    pallas_call x2, Pallas kernels, head_call(): pl.pallas_call(functools.partial(body, per_step), out_shape=out, grid_spe...  17 us
    ppermute x6, starting transfers between devices, send_up(): came.append(lax.ppermute(up, 'ctx', up_pairs(self.n_ctx, self.plane, r)))  13.3 us
    ppermute x6, starting transfers between devices, send_in(): piece = lax.ppermute(piece, 'ctx', plane_pairs(self.n_ctx, self.plane, k))  9.43 us
    convert_element_type x8, other arithmetic, add_all(): return total.astype(dtype)  8.85 us
    ppermute x6, waiting for transfers between devices, send_in(): piece = lax.ppermute(piece, 'ctx', plane_pairs(self.n_ctx, self.plane, k))  8.69 us
  transfers between devices with their start and end apart: 49, of which 16 were waited for; matrix products, arithmetic and copies ran while one was open for 5% of the time, Pallas kernels for 28%

profile of v2, /device:TPU:0, one launch (start us, length us, event | category | flops | bytes accessed | tf_op | source)
XLA Modules:
  0.0 307.3 jit_solution(18188577154811360023)
XLA Ops:
  2.8 2.4 copy_bitcast_fusion
  5.2 4.0 %prep.1 = (bf16[8,256,128]{2,1,0:T(8,128)(2,1)}, f32[264,128]{1,0:T(8,128)}, f32[264,128]{1,0:T(8,128)}, f32[264,128]{1,0:T(8,128)}, f32[264,128]{1,0:T(8,128)},...) custom-call(s32[1]{0:T(128)} %bitcast.mine_ref, ...), custom_call_target="tpu_custom_call" | custom-call | flops 268435456 | bytes 2097152 | tf_op jit(solution)/shard_map/prep/pallas_call | solution.py:302
  9.1 3.0 collective-permute-start
  16.4 3.0 collective-permute-done.1.refs_2_.refs_6_
  23.2 3.5 %collective-permute-start.3 = (f32[264,128]{1,0:T(8,128)}, f32[264,128]{1,0:T(8,128)S(1)}, u32[]{:S(2)}, u32[]{:S(2)}) collective-permute-start(f32[264,128]{1,0:T(8,128)} %shard_map.140), channel_id=1, source_target_pairs={{0,8},{2,10},{4,12},{6,14},{8,16},{10,18},{12,20},{14,22},{16,24},... | collective-permute-start | bytes 405512 | tf_op jit(solution)/shard_map/ppermute | solution.py:463
  26.7 4.5 %collective-permute-start.4 = (f32[264,128]{1,0:T(8,128)}, f32[264,128]{1,0:T(8,128)S(1)}, u32[]{:S(2)}, u32[]{:S(2)}) collective-permute-start(f32[264,128]{1,0:T(8,128)} %shard_map.140), channel_id=1, source_target_pairs={{0,16},{2,18},{4,20},{6,22},{8,24},{10,26},{12,28},{14,30},{1,17},... | collective-permute-start | bytes 405512 | tf_op jit(solution)/shard_map/ppermute | solution.py:463
  61.5 12.0 %shard_map.142.answer_ref = f32[8,256,128]{2,1,0:T(8,128)} custom-call(s32[1]{0:T(128)} %bitcast.mine_ref, bf16[8,256,128]{2,1,0:T(8,128)(2,1)} %bitcast.37, bf16[8,256,128]{2,1,0:T(8,128)(2,1)} %get-tuple-element.27.unit_ref, f32[8,1,256]{2,1,0:T(1,128)} %bitcast.38, f32[8,1,128]{2,1,0:T(1,128)} %bitcast.41, f32[256,128]{1,0:T(8,128)} %get-tuple-element.32.refs_0_, ...), custom_call_target="tpu_custom_call" | custom-call | flops 2952790016 | bytes 3145728 | tf_op jit(solution)/shard_map/pallas_call | solution.py:569
  74.2 5.0 %shard_map.145 = bf16[256,1024]{1,0:T(8,128)(2,1)} custom-call(s32[1]{0:T(128)} %bitcast.mine_ref, f32[8,256,128]{2,1,0:T(8,128)} %shard_map.142.answer_ref, bf16[8,256,128]{2,1,0:T(8,128)(2,1)} %get-tuple-element.27.unit_ref, bf16[8,256,128]{2,1,0:T(8,128)(2,1)} %get-tuple-element.56.value_ref, f32[8,1,256]{2,1,0:T(1,128)} %bitcast.39, ...), custom_call_target="tpu_custom_call" | custom-call | flops 671088640 | bytes 3145728 | tf_op jit(solution)/shard_map/pallas_call | solution.py:569
  79.2 3.7 %fusion.12 = f32[256,2048]{1,0:T(8,128)S(1)} fusion(bf16[256,1024]{1,0:T(8,128)(2,1)} %shard_map.145, bf16[1024,2048]{1,0:T(8,128)(2,1)} %param.19), kind=kOutput, calls=%fused_computation.40 | convolution fusion | flops 1073741824 | bytes 6815744 | tf_op jit(solution)/shard_map/dot_general | solution.py:654
  89.8 13.5 %collective-permute-done.36.refs_0_ = bf16[128,2048]{1,0:T(8,128)(2,1)} collective-permute-done((bf16[128,2048]{1,0:T(8,128)(2,1)S(1)}, bf16[128,2048]{1,0:T(8,128)(2,1)}, u32[]{:S(2)}, u32[]{:S(2)}) %collective-permute-start.36) | collective-permute-done | bytes 524320 | tf_op jit(solution)/shard_map/ppermute | solution.py:45
  103.3 22.4 %collective-permute-start.19 = (bf16[128,2048]{1,0:T(8,128)(2,1)S(1)}, bf16[128,2048]{1,0:T(8,128)(2,1)}, u32[]{:S(2)}, u32[]{:S(2)}) collective-permute-start(bf16[128,2048]{1,0:T(8,128)(2,1)S(1)} %fusion.2.refs_0_), channel_id=1, source_target_pairs={{0,8},{1,9},{2,10},{3,11},{4,12},{5,13},{6,14},{7,15},{8,16},{9,17... | collective-permute-start | bytes 1572872 | tf_op jit(solution)/shard_map/ppermute | solution.py:45
  125.7 9.8 %collective-permute-done.29.refs_0_ = bf16[128,2048]{1,0:T(8,128)(2,1)} collective-permute-done((bf16[128,2048]{1,0:T(8,128)(2,1)S(1)}, bf16[128,2048]{1,0:T(8,128)(2,1)}, u32[]{:S(2)}, u32[]{:S(2)}) %collective-permute-start.29) | collective-permute-done | bytes 524320 | tf_op jit(solution)/shard_map/ppermute | solution.py:45
  137.9 11.7 %collective-permute-done.37.refs_1_ = bf16[128,2048]{1,0:T(8,128)(2,1)} collective-permute-done((bf16[128,2048]{1,0:T(8,128)(2,1)}, bf16[128,2048]{1,0:T(8,128)(2,1)}, u32[]{:S(2)}, u32[]{:S(2)}) %collective-permute-start.37) | collective-permute-done | bytes 524320 | tf_op jit(solution)/shard_map/ppermute | solution.py:45
  151.7 3.7 %all-to-all-start = ((f32[16,2,128]{2,1,0:T(2,128)}), f32[16,2,128]{2,1,0:T(2,128)S(1)}, u32[]{:S(2)}, u32[]{:S(2)}) async-start(f32[16,2,128]{2,1,0:T(2,128)} %bitcast.13), calls=%async_computation | async-start | bytes 32768 | tf_op jit(solution)/shard_map/all_to_all | solution.py:665
  163.3 7.2 %collective-permute-done.20.refs_1_ = bf16[128,2048]{1,0:T(8,128)(2,1)} collective-permute-done((bf16[128,2048]{1,0:T(8,128)(2,1)}, bf16[128,2048]{1,0:T(8,128)(2,1)}, u32[]{:S(2)}, u32[]{:S(2)}) %collective-permute-start.20) | collective-permute-done | bytes 524320 | tf_op jit(solution)/shard_map/ppermute | solution.py:45
  171.9 3.1 %collective-permute-done.39.refs_3_ = bf16[128,2048]{1,0:T(8,128)(2,1)} collective-permute-done((bf16[128,2048]{1,0:T(8,128)(2,1)}, bf16[128,2048]{1,0:T(8,128)(2,1)}, u32[]{:S(2)}, u32[]{:S(2)}) %collective-permute-start.39) | collective-permute-done | bytes 524320 | tf_op jit(solution)/shard_map/ppermute | solution.py:45
  179.8 17.0 %shard_map.148 = (bf16[256,2048]{1,0:T(8,128)(2,1)}, bf16[256,2048]{1,0:T(8,128)(2,1)}) custom-call(s32[4]{0:T(128)} %pad_add_fusion.2.src_ref, s32[16,2,128]{2,1,0:T(2,128)} %fusion.10.slot_ref, f32[16,2,128]{2,1,0:T(2,128)} %get-tuple-element.55.gate_ref, bf16[128,2048]{1,0:T(8,128)(2,1)} %collective-permute-done.36.refs_0_, ...), custom_call_target="tpu_custom_call" | custom-call | flops 4831838208 | bytes 23068672 | tf_op jit(solution)/shard_map/pallas_call | solution.py:214
  199.7 16.8 %shard_map.147 = (bf16[256,2048]{1,0:T(8,128)(2,1)}, bf16[256,2048]{1,0:T(8,128)(2,1)}) custom-call(s32[4]{0:T(128)} %pad_add_fusion.1.src_ref, s32[16,2,128]{2,1,0:T(2,128)} %fusion.10.slot_ref, f32[16,2,128]{2,1,0:T(2,128)} %get-tuple-element.55.gate_ref, bf16[128,2048]{1,0:T(8,128)(2,1)} %collective-permute-done.29.refs_0_, ...), custom_call_target="tpu_custom_call" | custom-call | flops 4831838208 | bytes 23068672 | tf_op jit(solution)/shard_map/pallas_call | solution.py:214
  218.6 17.1 %shard_map.146 = (bf16[256,2048]{1,0:T(8,128)(2,1)}, bf16[256,2048]{1,0:T(8,128)(2,1)}) custom-call(s32[4]{0:T(128)} %pad_add_fusion.src_ref, s32[16,2,128]{2,1,0:T(2,128)} %fusion.10.slot_ref, f32[16,2,128]{2,1,0:T(2,128)} %get-tuple-element.55.gate_ref, bf16[128,2048]{1,0:T(8,128)(2,1)} %collective-permute-done.19.refs_0_, ...), custom_call_target="tpu_custom_call" | custom-call | flops 4831838208 | bytes 23068672 | tf_op jit(solution)/shard_map/pallas_call | solution.py:214
  237.4 16.9 %shard_map.149 = (bf16[256,2048]{1,0:T(8,128)(2,1)}, bf16[256,2048]{1,0:T(8,128)(2,1)}) custom-call(s32[4]{0:T(128)} %pad_add_fusion.3.src_ref, s32[16,2,128]{2,1,0:T(2,128)} %fusion.10.slot_ref, f32[16,2,128]{2,1,0:T(2,128)} %get-tuple-element.55.gate_ref, bf16[128,2048]{1,0:T(8,128)(2,1)} %copy-done.6, bf16[128,2048]{1,0:T(8,128)(2,1)} %copy-done.16, ...), custom_call_target="tpu_custom_call" | custom-call | flops 4831838208 | bytes 23068672 | tf_op jit(solution)/shard_map/pallas_call | solution.py:214
  262.9 17.7 %collective-permute-done.46 = bf16[256,2048]{1,0:T(8,128)(2,1)S(1)} collective-permute-done((bf16[256,2048]{1,0:T(8,128)(2,1)}, bf16[256,2048]{1,0:T(8,128)(2,1)S(1)}, u32[]{:S(2)}, u32[]{:S(2)}) %collective-permute-start.46) | collective-permute-done | bytes 1048608 | tf_op jit(solution)/shard_map/ppermute | solution.py:45
  287.0 3.2 %collective-permute-start.28 = (bf16[128,2048]{1,0:T(8,128)(2,1)S(1)}, bf16[128,2048]{1,0:T(8,128)(2,1)S(1)}, u32[]{:S(2)}, u32[]{:S(2)}) collective-permute-start(bf16[128,2048]{1,0:T(8,128)(2,1)S(1)} %add_convert_fusion.6), channel_id=1, source_target_pairs={{0,24},{1,25},{2,26},{3,27},{4,28},{5,29},{6,30},{7,31},{8,0},{9,1... | collective-permute-start | bytes 1572872 | tf_op jit(solution)/shard_map/ppermute | solution.py:45
  290.2 4.6 %collective-permute-done.42 = bf16[128,2048]{1,0:T(8,128)(2,1)S(1)} collective-permute-done((bf16[128,2048]{1,0:T(8,128)(2,1)S(1)}, bf16[128,2048]{1,0:T(8,128)(2,1)S(1)}, u32[]{:S(2)}, u32[]{:S(2)}) %collective-permute-start.42) | collective-permute-done | bytes 524320 | tf_op jit(solution)/shard_map/ppermute | solution.py:45
  294.9 11.1 %collective-permute-done.35 = bf16[128,2048]{1,0:T(8,128)(2,1)S(1)} collective-permute-done((bf16[128,2048]{1,0:T(8,128)(2,1)S(1)}, bf16[128,2048]{1,0:T(8,128)(2,1)S(1)}, u32[]{:S(2)}, u32[]{:S(2)}) %collective-permute-start.35) | collective-permute-done | bytes 524320 | tf_op jit(solution)/shard_map/ppermute | solution.py:45
  (190 shorter events, 89.0 us)
Async XLA Ops:
  13.6 20.0 %collective-permute-start.9 = (bf16[256,128]{1,0:T(8,128)(2,1)}, bf16[256,128]{1,0:T(8,128)(2,1)S(1)}, u32[]{:S(2)}, u32[]{:S(2)}) collective-permute-start(bf16[256,128]{1,0:T(8,128)(2,1)} %get-tuple-element.37), channel_id=1, source_target_pairs={{0,2},{2,0},{4,6},{6,4},{8,10},{10,8},{12,14},{14,12},{16,18},{18,... | collective-permute-start | bytes 196616 | tf_op jit(solution)/shard_map/ppermute | solution.py:442
  23.2 20.7 %collective-permute-start.3 = (f32[264,128]{1,0:T(8,128)}, f32[264,128]{1,0:T(8,128)S(1)}, u32[]{:S(2)}, u32[]{:S(2)}) collective-permute-start(f32[264,128]{1,0:T(8,128)} %shard_map.140), channel_id=1, source_target_pairs={{0,8},{2,10},{4,12},{6,14},{8,16},{10,18},{12,20},{14,22},{16,24},... | collective-permute-start | bytes 405512 | tf_op jit(solution)/shard_map/ppermute | solution.py:463
  83.9 92.1 %collective-permute-start.23 = (bf16[1,2048,768]{2,1,0:T(8,128)(2,1)S(1)}, bf16[1,2048,768]{2,1,0:T(8,128)(2,1)}, u32[]{:S(2)}, u32[]{:S(2)}) collective-permute-start(bf16[1,2048,768]{2,1,0:T(8,128)(2,1)S(1)} %copy-done), channel_id=1, source_target_pairs={{0,1},{1,0},{2,3},{3,2},{4,5},{5,4},{6,7},{7,6},{8,9},{9,8},{10,11... | collective-permute-start | bytes 9437192 | tf_op jit(solution)/shard_map/ppermute | solution.py:612
  84.4 93.3 %collective-permute-start.24 = (bf16[1,2048,768]{2,1,0:T(8,128)(2,1)}, bf16[1,2048,768]{2,1,0:T(8,128)(2,1)}, u32[]{:S(2)}, u32[]{:S(2)}) collective-permute-start(bf16[1,2048,768]{2,1,0:T(8,128)(2,1)} %refs_5_.7), channel_id=1, source_target_pairs={{0,1},{1,0},{2,3},{3,2},{4,5},{5,4},{6,7},{7,6},{8,9},{9,8},{10,11... | collective-permute-start | bytes 9437192 | tf_op jit(solution)/shard_map/ppermute | solution.py:612
  84.4 94.1 %collective-permute-start.25 = (bf16[1,768,2048]{2,1,0:T(8,128)(2,1)}, bf16[1,768,2048]{2,1,0:T(8,128)(2,1)}, u32[]{:S(2)}, u32[]{:S(2)}) collective-permute-start(bf16[1,768,2048]{2,1,0:T(8,128)(2,1)} %refs_6_.7), channel_id=1, source_target_pairs={{0,1},{1,0},{2,3},{3,2},{4,5},{5,4},{6,7},{7,6},{8,9},{9,8},{10,11... | collective-permute-start | bytes 9437192 | tf_op jit(solution)/shard_map/ppermute | solution.py:612
  89.0 46.5 %collective-permute-start.29 = (bf16[128,2048]{1,0:T(8,128)(2,1)S(1)}, bf16[128,2048]{1,0:T(8,128)(2,1)}, u32[]{:S(2)}, u32[]{:S(2)}) collective-permute-start(bf16[128,2048]{1,0:T(8,128)(2,1)S(1)} %fusion.2.refs_0_), channel_id=1, source_target_pairs={{0,16},{1,17},{2,18},{3,19},{4,20},{5,21},{6,22},{7,23},{8,24},{9,... | collective-permute-start | bytes 1572872 | tf_op jit(solution)/shard_map/ppermute | solution.py:45
  103.3 33.1 %collective-permute-start.19 = (bf16[128,2048]{1,0:T(8,128)(2,1)S(1)}, bf16[128,2048]{1,0:T(8,128)(2,1)}, u32[]{:S(2)}, u32[]{:S(2)}) collective-permute-start(bf16[128,2048]{1,0:T(8,128)(2,1)S(1)} %fusion.2.refs_0_), channel_id=1, source_target_pairs={{0,8},{1,9},{2,10},{3,11},{4,12},{5,13},{6,14},{7,15},{8,16},{9,17... | collective-permute-start | bytes 1572872 | tf_op jit(solution)/shard_map/ppermute | solution.py:45
  136.4 21.1 %collective-permute-start.38 = (bf16[128,2048]{1,0:T(8,128)(2,1)}, bf16[128,2048]{1,0:T(8,128)(2,1)}, u32[]{:S(2)}, u32[]{:S(2)}) collective-permute-start(bf16[128,2048]{1,0:T(8,128)(2,1)} %collective-permute-done.36.refs_0_), channel_id=1, source_target_pairs={{0,4},{1,3},{2,6},{3,1},{4,0},{5,7},{6,2},{7,5},{8,12},{9,11},{10,... | collective-permute-start | bytes 1572872 | tf_op jit(solution)/shard_map/ppermute | solution.py:45
  170.5 26.2 %collective-permute-start.43 = (bf16[128,2048]{1,0:T(8,128)(2,1)}, bf16[128,2048]{1,0:T(8,128)(2,1)S(1)}, u32[]{:S(2)}, u32[]{:S(2)}) collective-permute-start(bf16[128,2048]{1,0:T(8,128)(2,1)} %copy-done.6), channel_id=1, source_target_pairs={{0,2},{1,5},{2,0},{3,7},{4,6},{5,1},{6,4},{7,3},{8,10},{9,13},{10,... | collective-permute-start | bytes 1572872 | tf_op jit(solution)/shard_map/ppermute | solution.py:45
  175.1 22.6 %collective-permute-start.31 = (bf16[128,2048]{1,0:T(8,128)(2,1)}, bf16[128,2048]{1,0:T(8,128)(2,1)}, u32[]{:S(2)}, u32[]{:S(2)}) collective-permute-start(bf16[128,2048]{1,0:T(8,128)(2,1)} %collective-permute-done.29.refs_0_), channel_id=1, source_target_pairs={{0,4},{1,3},{2,6},{3,1},{4,0},{5,7},{6,2},{7,5},{8,12},{9,11},{10,... | collective-permute-start | bytes 1572872 | tf_op jit(solution)/shard_map/ppermute | solution.py:45
  175.9 22.9 %collective-permute-start.32 = (bf16[128,2048]{1,0:T(8,128)(2,1)}, bf16[128,2048]{1,0:T(8,128)(2,1)S(1)}, u32[]{:S(2)}, u32[]{:S(2)}) collective-permute-start(bf16[128,2048]{1,0:T(8,128)(2,1)} %collective-permute-done.30.refs_1_), channel_id=1, source_target_pairs={{0,4},{1,3},{2,6},{3,1},{4,0},{5,7},{6,2},{7,5},{8,12},{9,11},{10,... | collective-permute-start | bytes 1572872 | tf_op jit(solution)/shard_map/ppermute | solution.py:45
  177.7 38.8 %collective-permute-start.21 = (bf16[128,2048]{1,0:T(8,128)(2,1)}, bf16[128,2048]{1,0:T(8,128)(2,1)S(1)}, u32[]{:S(2)}, u32[]{:S(2)}) collective-permute-start(bf16[128,2048]{1,0:T(8,128)(2,1)} %collective-permute-done.19.refs_0_), channel_id=1, source_target_pairs={{0,4},{1,3},{2,6},{3,1},{4,0},{5,7},{6,2},{7,5},{8,12},{9,11},{10,... | collective-permute-start | bytes 1572872 | tf_op jit(solution)/shard_map/ppermute | solution.py:45
  178.6 39.2 %collective-permute-start.22 = (bf16[128,2048]{1,0:T(8,128)(2,1)}, bf16[128,2048]{1,0:T(8,128)(2,1)S(1)}, u32[]{:S(2)}, u32[]{:S(2)}) collective-permute-start(bf16[128,2048]{1,0:T(8,128)(2,1)} %collective-permute-done.20.refs_1_), channel_id=1, source_target_pairs={{0,4},{1,3},{2,6},{3,1},{4,0},{5,7},{6,2},{7,5},{8,12},{9,11},{10,... | collective-permute-start | bytes 1572872 | tf_op jit(solution)/shard_map/ppermute | solution.py:45
  196.7 39.9 %collective-permute-start.44 = (bf16[128,2048]{1,0:T(8,128)(2,1)S(1)}, bf16[128,2048]{1,0:T(8,128)(2,1)S(1)}, u32[]{:S(2)}, u32[]{:S(2)}) collective-permute-start(bf16[128,2048]{1,0:T(8,128)(2,1)S(1)} %copy-done.7), channel_id=1, source_target_pairs={{0,4},{1,3},{2,6},{3,1},{4,0},{5,7},{6,2},{7,5},{8,12},{9,11},{10,... | collective-permute-start | bytes 1572872 | tf_op jit(solution)/shard_map/ppermute | solution.py:45
  197.7 39.0 %collective-permute-start.45 = (bf16[128,2048]{1,0:T(8,128)(2,1)S(1)}, bf16[128,2048]{1,0:T(8,128)(2,1)}, u32[]{:S(2)}, u32[]{:S(2)}) collective-permute-start(bf16[128,2048]{1,0:T(8,128)(2,1)S(1)} %collective-permute-done.43.refs_1_), channel_id=1, source_target_pairs={{0,4},{1,3},{2,6},{3,1},{4,0},{5,7},{6,2},{7,5},{8,12},{9,11},{10,... | collective-permute-start | bytes 1572872 | tf_op jit(solution)/shard_map/ppermute | solution.py:45
  198.8 56.7 %collective-permute-start.40 = (bf16[256,2048]{1,0:T(8,128)(2,1)}, bf16[256,2048]{1,0:T(8,128)(2,1)}, u32[]{:S(2)}, u32[]{:S(2)}) collective-permute-start(bf16[256,2048]{1,0:T(8,128)(2,1)} %get-tuple-element.49), channel_id=1, source_target_pairs={{0,4},{1,3},{2,6},{3,1},{4,0},{5,7},{6,2},{7,5},{8,12},{9,11},{10,... | collective-permute-start | bytes 3145736 | tf_op jit(solution)/shard_map/ppermute | solution.py:45
  216.5 41.8 %collective-permute-start.33 = (bf16[256,2048]{1,0:T(8,128)(2,1)}, bf16[256,2048]{1,0:T(8,128)(2,1)}, u32[]{:S(2)}, u32[]{:S(2)}) collective-permute-start(bf16[256,2048]{1,0:T(8,128)(2,1)} %get-tuple-element.47), channel_id=1, source_target_pairs={{0,4},{1,3},{2,6},{3,1},{4,0},{5,7},{6,2},{7,5},{8,12},{9,11},{10,... | collective-permute-start | bytes 3145736 | tf_op jit(solution)/shard_map/ppermute | solution.py:45
  235.7 24.4 %collective-permute-start.26 = (bf16[256,2048]{1,0:T(8,128)(2,1)}, bf16[256,2048]{1,0:T(8,128)(2,1)}, u32[]{:S(2)}, u32[]{:S(2)}) collective-permute-start(bf16[256,2048]{1,0:T(8,128)(2,1)} %get-tuple-element.45), channel_id=1, source_target_pairs={{0,4},{1,3},{2,6},{3,1},{4,0},{5,7},{6,2},{7,5},{8,12},{9,11},{10,... | collective-permute-start | bytes 3145736 | tf_op jit(solution)/shard_map/ppermute | solution.py:45
  254.3 26.3 %collective-permute-start.46 = (bf16[256,2048]{1,0:T(8,128)(2,1)}, bf16[256,2048]{1,0:T(8,128)(2,1)S(1)}, u32[]{:S(2)}, u32[]{:S(2)}) collective-permute-start(bf16[256,2048]{1,0:T(8,128)(2,1)} %get-tuple-element.51), channel_id=1, source_target_pairs={{0,4},{1,3},{2,6},{3,1},{4,0},{5,7},{6,2},{7,5},{8,12},{9,11},{10,... | collective-permute-start | bytes 3145736 | tf_op jit(solution)/shard_map/ppermute | solution.py:45
  256.7 25.6 %collective-permute-start.41 = (bf16[128,2048]{1,0:T(8,128)(2,1)S(1)}, bf16[128,2048]{1,0:T(8,128)(2,1)S(1)}, u32[]{:S(2)}, u32[]{:S(2)}) collective-permute-start(bf16[128,2048]{1,0:T(8,128)(2,1)S(1)} %add_convert_fusion.3), channel_id=1, source_target_pairs={{0,2},{1,5},{2,0},{3,7},{4,6},{5,1},{6,4},{7,3},{8,10},{9,13},{10,... | collective-permute-start | bytes 1572872 | tf_op jit(solution)/shard_map/ppermute | solution.py:45
  259.6 24.1 %collective-permute-start.34 = (bf16[128,2048]{1,0:T(8,128)(2,1)S(1)}, bf16[128,2048]{1,0:T(8,128)(2,1)S(1)}, u32[]{:S(2)}, u32[]{:S(2)}) collective-permute-start(bf16[128,2048]{1,0:T(8,128)(2,1)S(1)} %add_convert_fusion.5), channel_id=1, source_target_pairs={{0,2},{1,5},{2,0},{3,7},{4,6},{5,1},{6,4},{7,3},{8,10},{9,13},{10,... | collective-permute-start | bytes 1572872 | tf_op jit(solution)/shard_map/ppermute | solution.py:45
  261.2 24.5 %collective-permute-start.27 = (bf16[128,2048]{1,0:T(8,128)(2,1)S(1)}, bf16[128,2048]{1,0:T(8,128)(2,1)S(1)}, u32[]{:S(2)}, u32[]{:S(2)}) collective-permute-start(bf16[128,2048]{1,0:T(8,128)(2,1)S(1)} %add_convert_fusion.7), channel_id=1, source_target_pairs={{0,2},{1,5},{2,0},{3,7},{4,6},{5,1},{6,4},{7,3},{8,10},{9,13},{10,... | collective-permute-start | bytes 1572872 | tf_op jit(solution)/shard_map/ppermute | solution.py:45
  285.0 20.9 %collective-permute-start.35 = (bf16[128,2048]{1,0:T(8,128)(2,1)S(1)}, bf16[128,2048]{1,0:T(8,128)(2,1)S(1)}, u32[]{:S(2)}, u32[]{:S(2)}) collective-permute-start(bf16[128,2048]{1,0:T(8,128)(2,1)S(1)} %add_convert_fusion.4), channel_id=1, source_target_pairs={{0,16},{1,17},{2,18},{3,19},{4,20},{5,21},{6,22},{7,23},{8,24},{9,... | collective-permute-start | bytes 1572872 | tf_op jit(solution)/shard_map/ppermute | solution.py:45
  287.0 18.9 %collective-permute-start.28 = (bf16[128,2048]{1,0:T(8,128)(2,1)S(1)}, bf16[128,2048]{1,0:T(8,128)(2,1)S(1)}, u32[]{:S(2)}, u32[]{:S(2)}) collective-permute-start(bf16[128,2048]{1,0:T(8,128)(2,1)S(1)} %add_convert_fusion.6), channel_id=1, source_target_pairs={{0,24},{1,25},{2,26},{3,27},{4,28},{5,29},{6,30},{7,31},{8,0},{9,1... | collective-permute-start | bytes 1572872 | tf_op jit(solution)/shard_map/ppermute | solution.py:45
  (62 other events, 652.1 us)
